TPU v7x, 256 devices: a whole 4x4x8 slice. The times are simulated.
256 devices in a mesh: user: 8 (over x, core), item: 32 (over y, z).
Axes of the slice: x: 4, y: 4, z: 8, core: 2. Of those that a mesh axis runs over, the one named last changes fastest.
Arguments:
- user_factors: float32 [65536, 256], P(('user', 'item')), may hold values from -6 to 6
- item_factors: bfloat16 [131072, 256], P('item')
- head_ids: int32 [8], replicated, may hold values from 0 to 511, as said below
- tail_ids: int32 [256, 16], P(('user', 'item')), may hold values from 0 to 511, as said below
- head_counts: int32 [256, 8, 256, 256], P(('user', 'item')), may hold values from 0 to 7
- tail_counts: int32 [256, 16, 256, 256], P(('user', 'item')), may hold values from 0 to 7
Outputs:
- new_factors: float32 [65536, 256], P(('user', 'item'))
- residual: float32 [65536, 256], P(('user', 'item'))
Inputs may be any that keep to these rules, and one draw needn't show every extreme that they name: `head_ids`: 8 distinct block numbers, among them 0 and 511. `tail_ids`: each row holds distinct block numbers; at most 1 of a row fall in the range of one index of item (blocks o * 16 to (o + 1) * 16 - 1), and one range, the same for every row, holds exactly 1 of every row.
All inputs are finite; a program needn't handle non-finite values.
Results may differ from a plain program's by a relative error of at most 0.0055.
Values may be sent and summed in bfloat16 or wider, within the bound.
No kernel may reach another device: no remote copies, remote signals or barrier semaphores. Data moves between devices by JAX's collectives and lax.ppermute only.
A program may use at most 128 MiB of HBM per device.

v0:
```python
import jax
import jax.numpy as jnp
from jax import lax
from jax.sharding import PartitionSpec as P

ITERS = 2


conf_alpha = 4.0
ridge_term = 0.1
epsilon = 1e-06


def broadcast(shard, axis, root):
    mine = lax.axis_index(axis) == root
    return lax.psum(jnp.where(mine, shard, jnp.zeros_like(shard)), axis)


def apply_operator(vector, gram_matrix, item_tiles, weights):
    rounded = vector.astype(jnp.bfloat16)
    scores = jnp.einsum("uf,kif->kui", rounded, item_tiles, preferred_element_type=jnp.float32)
    scaled = (scores * weights).astype(jnp.bfloat16)
    data_term = jnp.einsum("kui,kif->uf", scaled, item_tiles, preferred_element_type=jnp.float32)
    gram_term = jnp.dot(vector, gram_matrix, precision=lax.Precision.HIGHEST)
    return gram_term + ridge_term * vector + data_term


def solve_block(start_vec, gram_matrix, item_tiles, counts):
    count_float = counts.astype(jnp.float32)
    weights = (conf_alpha * count_float).astype(jnp.bfloat16)
    rated_weight = jnp.where(counts > 0, 1.0 + conf_alpha * count_float, 0.0).astype(jnp.bfloat16)
    rhs = jnp.einsum("kui,kif->uf", rated_weight, item_tiles, preferred_element_type=jnp.float32)
    solution = start_vec
    residual = rhs - apply_operator(solution, gram_matrix, item_tiles, weights)
    direction = residual
    norm_now = jnp.sum(residual * residual, axis=1, keepdims=True)
    for turn_index in range(ITERS):
        image_vec = apply_operator(direction, gram_matrix, item_tiles, weights)
        step_size = norm_now / (jnp.sum(direction * image_vec, axis=1, keepdims=True) + epsilon)
        solution = solution + step_size * direction
        residual = residual - step_size * image_vec
        if turn_index + 1 < ITERS:
            norm_next = jnp.sum(residual * residual, axis=1, keepdims=True)
            direction = residual + norm_next / (norm_now + epsilon) * direction
            norm_now = norm_next
    return (solution, residual)


def local(user_factors, item_factors, head_ids, tail_ids, head_counts, tail_counts):
    item_count = lax.axis_size("item")
    user_count = lax.axis_size("user")
    block_size = head_counts.shape[-1]
    rank_width = item_factors.shape[1]
    shard_blocks = item_factors.shape[0] // block_size
    blocks = item_factors.reshape(shard_blocks, block_size, rank_width)
    contract = (((0,), (0,)), ((), ()))
    slice_rows = item_factors.shape[0] // user_count
    rows_part = lax.dynamic_slice_in_dim(
        item_factors, lax.axis_index("user") * slice_rows, slice_rows, 0
    )
    local_gram = lax.dot_general(rows_part, rows_part, contract, preferred_element_type=jnp.float32)
    gram_matrix = lax.psum(local_gram, ("user", "item"))
    head_owner = head_ids // shard_blocks
    head_local = head_ids % shard_blocks
    head_total = head_ids.shape[0]

    def take_turn(index, gathered):
        block_rows = lax.dynamic_index_in_dim(blocks, head_local[index], 0, keepdims=False)
        arrived = broadcast(block_rows, "item", head_owner[index])
        return lax.dynamic_update_index_in_dim(gathered, arrived, index, 0)

    empty = jnp.zeros((head_total, block_size, rank_width), jnp.bfloat16)
    head_rows = lax.fori_loop(0, head_total, take_turn, empty)
    wanted = tail_ids.reshape(-1)
    length = wanted.shape[0]
    capacity = 2 * length // item_count
    owner_of = wanted // shard_blocks
    local_of = wanted % shard_blocks
    same_owner = owner_of[:, None] == owner_of[None, :]
    positions = jnp.arange(length, dtype=jnp.int32)
    earlier = positions[:, None] > positions[None, :]
    place_index = jnp.sum((same_owner & earlier).astype(jnp.int32), axis=1)
    slot_index = owner_of * capacity + place_index
    slot_table = slot_index[:, None] == jnp.arange(item_count * capacity, dtype=jnp.int32)[None, :]
    requests = jnp.sum(jnp.where(slot_table, local_of[:, None], 0), axis=0)
    requests = requests.reshape(item_count, capacity)
    served = blocks[lax.all_to_all(requests, "item", split_axis=0, concat_axis=0, tiled=True)]
    arrived_tail = lax.all_to_all(served, "item", split_axis=0, concat_axis=0, tiled=True)
    tail_rows = arrived_tail.reshape(item_count * capacity, block_size, rank_width)[slot_index]
    local_blocks = tail_ids.shape[0]
    tail_tiles = tail_rows.reshape(local_blocks, tail_ids.shape[1], block_size, rank_width)
    start_blocks = user_factors.reshape(local_blocks, block_size, rank_width)

    def one_block(block_args):
        start_vec, tail_part_rows, head_part, tail_part = block_args
        item_tiles = jnp.concatenate([head_rows, tail_part_rows], axis=0)
        counts = jnp.concatenate([head_part, tail_part], axis=0)
        return solve_block(start_vec, gram_matrix, item_tiles, counts)

    solution, residual = lax.map(one_block, (start_blocks, tail_tiles, head_counts, tail_counts))
    return (
        solution.reshape(local_blocks * block_size, rank_width),
        residual.reshape(local_blocks * block_size, rank_width),
    )


def solution(mesh):
    return jax.shard_map(
        local,
        mesh=mesh,
        in_specs=(
            P(("user", "item"), None),
            P("item", None),
            P(),
            P(("user", "item"), None),
            P(("user", "item"), None, None, None),
            P(("user", "item"), None, None, None),
        ),
        out_specs=(P(("user", "item"), None), P(("user", "item"), None)),
        check_vma=False,
    )
```

profile of v0, /device:TPU:2, one launch (start us, length us, event | category | flops | bytes accessed | tf_op | source)
XLA Modules:
  0.0 1522.7 jit_solution(15008813980043057980)
XLA Ops:
  9.7 21.1 %all_to_all.14 = s32[32,1,1]{2,1,0:T(1,128)S(1)} all-to-all(s32[32,1,1]{2,1,0:T(1,128)S(1)} %copy.57), channel_id=1, replica_groups=mesh['user'=8,'item'=32] {'item'}, dimensions={0} | all-to-all | bytes 256 | tf_op jit(solution)/shard_map/all_to_all | solution.py:87
  31.5 4.4 gather_fusion
  35.8 5.0 all-to-all-start.1
  40.9 2.0 fusion.32
  42.9 1194.5 %while.8 = (s32[]{:T(128)}, bf16[8,256,256]{1,2,0:T(8,128)(2,1)}, s32[8]{0:T(128)S(1)}, s32[8]{0:T(128)S(1)}, bf16[16,256,256]{2,1,0:T(8,128)(2,1)}, /*index=5*/s32[]{:T(128)}, s32[]{:T(128)}, s32[]{:T(128)}, u32[]{:T(128)}) while((s32[]{:T(128)}, bf16[8,256,256]{1,2,0:T(8,128)(2,1)}, s32[8]{0:T(128)S(1)}, s32[8]{0:T(128)S(1)}, ...), condition=%wide.region_2.3_spmd, body=%wide.region_0.2_spmd.sunk | while | flops 131080 | bytes 1573101 | solution.py:73
  48.2 151.8 %all-reduce.5.cloned.1.call-done = bf16[1,256,256]{2,1,0:T(8,128)(2,1)} async-done(((bf16[1,256,256]{2,1,0:T(8,128)(2,1)}), bf16[1,256,256]{2,1,0:T(8,128)(2,1)}) %all-reduce.5.cloned.1.call-update) | async-done | bytes 131088 | tf_op jit(solution)/shard_map/while/body/eval_jaxpr/psum | solution.py:16
  205.3 1.6 dynamic-slice_select_fusion.2
  206.9 141.0 %all-reduce.5.cloned.1.call-done = bf16[1,256,256]{2,1,0:T(8,128)(2,1)} async-done(((bf16[1,256,256]{2,1,0:T(8,128)(2,1)}), bf16[1,256,256]{2,1,0:T(8,128)(2,1)}) %all-reduce.5.cloned.1.call-update) | async-done | bytes 131088 | tf_op jit(solution)/shard_map/while/body/eval_jaxpr/psum | solution.py:16
  353.3 1.6 dynamic-slice_select_fusion.2
  354.9 141.0 %all-reduce.5.cloned.1.call-done = bf16[1,256,256]{2,1,0:T(8,128)(2,1)} async-done(((bf16[1,256,256]{2,1,0:T(8,128)(2,1)}), bf16[1,256,256]{2,1,0:T(8,128)(2,1)}) %all-reduce.5.cloned.1.call-update) | async-done | bytes 131088 | tf_op jit(solution)/shard_map/while/body/eval_jaxpr/psum | solution.py:16
  502.8 141.0 %all-reduce.5.cloned.1.call-done = bf16[1,256,256]{2,1,0:T(8,128)(2,1)} async-done(((bf16[1,256,256]{2,1,0:T(8,128)(2,1)}), bf16[1,256,256]{2,1,0:T(8,128)(2,1)}) %all-reduce.5.cloned.1.call-update) | async-done | bytes 131088 | tf_op jit(solution)/shard_map/while/body/eval_jaxpr/psum | solution.py:16
  650.8 141.0 %all-reduce.5.cloned.1.call-done = bf16[1,256,256]{2,1,0:T(8,128)(2,1)} async-done(((bf16[1,256,256]{2,1,0:T(8,128)(2,1)}), bf16[1,256,256]{2,1,0:T(8,128)(2,1)}) %all-reduce.5.cloned.1.call-update) | async-done | bytes 131088 | tf_op jit(solution)/shard_map/while/body/eval_jaxpr/psum | solution.py:16
  798.7 141.0 %all-reduce.5.cloned.1.call-done = bf16[1,256,256]{2,1,0:T(8,128)(2,1)} async-done(((bf16[1,256,256]{2,1,0:T(8,128)(2,1)}), bf16[1,256,256]{2,1,0:T(8,128)(2,1)}) %all-reduce.5.cloned.1.call-update) | async-done | bytes 131088 | tf_op jit(solution)/shard_map/while/body/eval_jaxpr/psum | solution.py:16
  946.7 141.0 %all-reduce.5.cloned.1.call-done = bf16[1,256,256]{2,1,0:T(8,128)(2,1)} async-done(((bf16[1,256,256]{2,1,0:T(8,128)(2,1)}), bf16[1,256,256]{2,1,0:T(8,128)(2,1)}) %all-reduce.5.cloned.1.call-update) | async-done | bytes 131088 | tf_op jit(solution)/shard_map/while/body/eval_jaxpr/psum | solution.py:16
  1094.6 141.0 %all-reduce.5.cloned.1.call-done = bf16[1,256,256]{2,1,0:T(8,128)(2,1)} async-done(((bf16[1,256,256]{2,1,0:T(8,128)(2,1)}), bf16[1,256,256]{2,1,0:T(8,128)(2,1)}) %all-reduce.5.cloned.1.call-update) | async-done | bytes 131088 | tf_op jit(solution)/shard_map/while/body/eval_jaxpr/psum | solution.py:16
  1237.9 5.5 copy.56
  1243.4 1.9 copy.55
  1245.5 2.9 gather_fusion.1
  1248.3 2.4 copy.59
  1250.7 6.8 fusion.23
  1257.6 4.5 fusion.17
  1262.1 233.9 %all-reduce.3.cloned.1.call-done = f32[256,256]{1,0:T(8,128)} async-done(((f32[256,256]{1,0:T(8,128)}), f32[256,256]{1,0:T(8,128)}) %all-reduce.3.cloned.1.call-update) | async-done | bytes 262160 | tf_op jit(solution)/shard_map/psum | solution.py:62
  1497.6 7.6 fusion.26
  1506.0 6.9 fusion.29
  (95 shorter events, 39.9 us)
Async XLA Ops:
  35.8 7.0 copy-start.5
  35.8 1209.6 %all-to-all-start.1 = ((bf16[32,1,256,256]{3,2,1,0:T(8,128)(2,1)}), bf16[32,1,256,256]{3,2,1,0:T(8,128)(2,1)}, u32[]{:S(2)}, u32[]{:S(2)}) async-start(bf16[32,1,256,256]{3,2,1,0:T(8,128)(2,1)} %bitcast.94), calls=%async_computation.1 | async-start | bytes 8388608 | tf_op jit(solution)/shard_map/all_to_all | solution.py:88
  42.9 157.1 %all-reduce.5.cloned.1.call-start = ((), (), s32[]{:S(2)}) async-start(), calls=%async_computation.3 | async-start | bytes 262144 | tf_op jit(solution)/shard_map/while/body/eval_jaxpr/psum | solution.py:16
  201.7 146.3 %all-reduce.5.cloned.1.call-start = ((), (), s32[]{:S(2)}) async-start(), calls=%async_computation.3 | async-start | bytes 262144 | tf_op jit(solution)/shard_map/while/body/eval_jaxpr/psum | solution.py:16
  349.6 146.3 %all-reduce.5.cloned.1.call-start = ((), (), s32[]{:S(2)}) async-start(), calls=%async_computation.3 | async-start | bytes 262144 | tf_op jit(solution)/shard_map/while/body/eval_jaxpr/psum | solution.py:16
  497.6 146.3 %all-reduce.5.cloned.1.call-start = ((), (), s32[]{:S(2)}) async-start(), calls=%async_computation.3 | async-start | bytes 262144 | tf_op jit(solution)/shard_map/while/body/eval_jaxpr/psum | solution.py:16
  645.5 146.3 %all-reduce.5.cloned.1.call-start = ((), (), s32[]{:S(2)}) async-start(), calls=%async_computation.3 | async-start | bytes 262144 | tf_op jit(solution)/shard_map/while/body/eval_jaxpr/psum | solution.py:16
  793.5 146.3 %all-reduce.5.cloned.1.call-start = ((), (), s32[]{:S(2)}) async-start(), calls=%async_computation.3 | async-start | bytes 262144 | tf_op jit(solution)/shard_map/while/body/eval_jaxpr/psum | solution.py:16
  941.4 146.3 %all-reduce.5.cloned.1.call-start = ((), (), s32[]{:S(2)}) async-start(), calls=%async_computation.3 | async-start | bytes 262144 | tf_op jit(solution)/shard_map/while/body/eval_jaxpr/psum | solution.py:16
  1089.4 146.3 %all-reduce.5.cloned.1.call-start = ((), (), s32[]{:S(2)}) async-start(), calls=%async_computation.3 | async-start | bytes 262144 | tf_op jit(solution)/shard_map/while/body/eval_jaxpr/psum | solution.py:16
  1237.3 258.7 %all-reduce.3.cloned.1.call-start = ((), (), s32[]{:S(2)}) async-start(), calls=%async_computation.2 | async-start | bytes 524288 | tf_op jit(solution)/shard_map/psum | solution.py:62
  1237.9 5.5 copy-start.1
  1243.4 1.9 copy-start.3
  1243.4 2.0 copy-start.6
  1250.7 6.8 copy-start.2
  1497.6 7.6 copy-start
  1497.6 8.4 copy-start.4
Sparse Core Ops, SparseCore 0:
  48.3 151.6 all-reduce.4
  207.0 140.8 all-reduce.4
  355.0 140.8 all-reduce.4
  503.0 140.8 all-reduce.4
  650.9 140.8 all-reduce.4
  798.9 140.8 all-reduce.4
  946.8 140.8 all-reduce.4
  1094.8 140.8 all-reduce.4
Sparse Core Ops, SparseCore 1:
  1243.8 252.1 all-reduce.2
where the time goes:
time: 1520 us
  waiting for transfers between devices  1370 us (90%)
  local copies, waits for them, and re-layouts  41.4 us (3%)
  matrix products  30.6 us (2%)
  blocking collectives  21.1 us (1%)
  loops' own time  20.3 us (1%)
  between operations  15.7 us (1%)
    psum x8, waiting for transfers between devices, broadcast(): return lax.psum(jnp.where(mine, shard, jnp.zeros_like(shard)), axis)  1140 us
    psum x1, waiting for transfers between devices, local(): gram_matrix = lax.psum(local_gram, ('user', 'item'))  234 us
  transfers between devices with their start and end apart: 10, of which 9 were waited for; matrix products, arithmetic and copies ran while one was open for 4% of the time, Pallas kernels for 0%

commit v1 on v0

v1 whole, which is shorter than its diff:
```python
import jax
import jax.numpy as jnp
from jax import lax
from jax.experimental import pallas as pl
from jax.experimental.pallas import tpu as pltpu
from jax.sharding import Mesh, PartitionSpec as P

ITERS = 2

conf_alpha = 4.0
ridge_term = 0.1
epsilon = 1e-06

USER, Y_SIZE, Z_SIZE = 8, 4, 8
ALL = ("user", "y", "z")
PLANE = ("user", "y")
NEAR = (0, -1, 1)
FAR = (-2, 2, -3, 3, 4)
SLOT_OF_SHIFT = tuple((NEAR + FAR).index(s if s <= 4 else s - 8) for s in range(8))


def whole(array):
    return pl.BlockSpec(array.shape, lambda *_: (0,) * len(array.shape))


def bf16(*shape):
    return jax.ShapeDtypeStruct(shape, jnp.bfloat16)


def store_split(out, at, values):
    high = values.astype(jnp.bfloat16)
    out[at] = high
    out[at + 1] = (values - high.astype(jnp.float32)).astype(jnp.bfloat16)


def prepare_kernel(place, blocks, out, gram):
    total, block, width = blocks.shape
    band = block // USER
    row = pl.multiple_of(place[0] * band, band)
    for k in range(total):
        rows = blocks[k]
        part = lax.dot_general(rows, rows, (((0,), (0,)), ((), ())), preferred_element_type=jnp.float32)
        if k == 0:
            gram[...] = part
        else:
            gram[...] += part
        out[k] = blocks[k, pl.ds(row, band), :]
    store_split(out, total, gram[pl.ds(row, width // USER), :])


def prepare(blocks, user):
    total, block, width = blocks.shape
    out = bf16(total + 2, block // USER, width)
    return pl.pallas_call(
        prepare_kernel,
        name="prepare",
        grid_spec=pltpu.PrefetchScalarGridSpec(
            num_scalar_prefetch=1,
            grid=(1,),
            in_specs=[whole(blocks)],
            out_specs=whole(out),
            scratch_shapes=[pltpu.VMEM((width, width), jnp.float32)],
        ),
        out_shape=out,
    )(user.reshape(1), blocks)


def pick_near_kernel(wanted, place, own, down, up, out):
    z = place[0]
    band = own.shape[1]
    peers = out.shape[0]
    first = pl.program_id(0) * peers
    for p in range(peers):
        for slot, (source, offset) in enumerate(zip((own, down, up), NEAR)):
            out[p, slot * band : (slot + 1) * band, :] = source[wanted[first + p, (z + offset) & (Z_SIZE - 1)]]


def pick_near(wanted, z, pieces):
    _, band, width = pieces[0].shape
    out = bf16(wanted.shape[0], len(NEAR) * band, width)
    return pl.pallas_call(
        pick_near_kernel,
        name="pick_near",
        grid_spec=pltpu.PrefetchScalarGridSpec(
            num_scalar_prefetch=2,
            grid=(2,),
            in_specs=[whole(piece) for piece in pieces],
            out_specs=pl.BlockSpec((out.shape[0] // 2, *out.shape[1:]), lambda i, *_: (i, 0, 0)),
        ),
        out_shape=out,
    )(wanted, z.reshape(1), *pieces)


def pick_far_kernel(wanted, head_ids, place, *refs):
    pieces, (out, shared) = refs[:-2], refs[-2:]
    z = place[0]
    total, band, width = pieces[0].shape
    per_shard = total - 2
    heads = head_ids.shape[0]
    peers = out.shape[0]
    first = pl.program_id(0) * peers

    @pl.when(pl.program_id(0) == 0)
    def _():
        def one_head(h, carry):
            block = head_ids[h]
            shift = (block // per_shard - z) & (Z_SIZE - 1)
            for source, offset in zip(pieces, NEAR + FAR):

                @pl.when(shift == offset % Z_SIZE)
                def _():
                    shared[h] = source[block & (per_shard - 1)]

            return carry

        lax.fori_loop(0, heads, one_head, 0)
        gram = jnp.zeros((band, width), jnp.float32)
        for source in pieces:
            gram += source[per_shard].astype(jnp.float32) + source[per_shard + 1].astype(jnp.float32)
        store_split(shared, heads, gram)

    for p in range(peers):
        for slot, (source, offset) in enumerate(zip(pieces[len(NEAR) :], FAR)):
            out[p, slot * band : (slot + 1) * band, :] = source[wanted[first + p, (z + offset) & (Z_SIZE - 1)]]


def pick_far(wanted, head_ids, z, pieces):
    _, band, width = pieces[0].shape
    out = bf16(wanted.shape[0], len(FAR) * band, width)
    shared = bf16(head_ids.shape[0] + 2, band, width)
    return pl.pallas_call(
        pick_far_kernel,
        name="pick_far",
        grid_spec=pltpu.PrefetchScalarGridSpec(
            num_scalar_prefetch=3,
            grid=(4,),
            in_specs=[whole(piece) for piece in pieces],
            out_specs=(
                pl.BlockSpec((out.shape[0] // 4, *out.shape[1:]), lambda i, *_: (i, 0, 0)),
                whole(shared),
            ),
        ),
        out_shape=(out, shared),
    )(wanted, head_ids, z.reshape(1), *pieces)


def merge_kernel(slabs, place, own, above, across, below, out):
    heads = slabs.shape[0]
    pieces = (own, above, across, below)
    for h in range(heads):
        shift = (slabs[h] - place[0]) & (Y_SIZE - 1)
        for other, source in enumerate(pieces):

            @pl.when(shift == other)
            def _():
                out[h] = source[h]

    gram = jnp.zeros(out.shape[1:], jnp.float32)
    for source in pieces:
        gram += source[heads].astype(jnp.float32) + source[heads + 1].astype(jnp.float32)
    store_split(out, heads, gram)


def merge(slabs, y, pieces):
    return pl.pallas_call(
        merge_kernel,
        name="merge",
        grid_spec=pltpu.PrefetchScalarGridSpec(
            num_scalar_prefetch=2,
            grid=(1,),
            in_specs=[whole(piece) for piece in pieces],
            out_specs=whole(pieces[0]),
        ),
        out_shape=bf16(*pieces[0].shape),
    )(slabs, y.reshape(1), *pieces)


def solve_kernel(slab, slot, place, start, near, far, same, other, head_counts, tail_counts, new_out, res_out, tiles, weights, counts, halves, gram, acc, tile_sems, count_sems, gram_sems, head_sems):
    heads, tails = head_counts.shape[1], tail_counts.shape[1]
    total = heads + tails
    block, width = start.shape
    band = same.shape[2]

    gram_copies, head_copies = [], []
    x, core = place[0] // 2, place[0] % 2
    for i, source in enumerate((same, other)):
        for j in range(USER // 2):
            n = i * (USER // 2) + j
            user = ((x + j) & (USER // 2 - 1)) * 2 + (core if i == 0 else 1 - core)
            gram_copies.append(pltpu.make_async_copy(source.at[j, heads:], halves.at[:, user], gram_sems.at[n]))
            head_copies.append(pltpu.make_async_copy(source.at[j, :heads], tiles.at[:heads, user], head_sems.at[n]))
    count_copies = [pltpu.make_async_copy(head_counts.at[0, k], counts.at[k], count_sems.at[k]) for k in range(heads)]
    count_copies += [
        pltpu.make_async_copy(tail_counts.at[0, k], counts.at[heads + k], count_sems.at[heads + k]) for k in range(tails)
    ]

    def tail_copy(k, source, first, any_rows=False):
        row = 0 if any_rows else pl.multiple_of((slot[k] - first) * band, band)
        return pltpu.make_async_copy(
            source.at[:, 0 if any_rows else slab[k], pl.ds(row, band), :], tiles.at[heads + k], tile_sems.at[heads + k]
        )

    for copy in gram_copies:
        copy.start()
    for k in range(tails):

        @pl.when(slot[k] < len(NEAR))
        def _():
            tail_copy(k, near, 0).start()

        @pl.when(slot[k] >= len(NEAR))
        def _():
            tail_copy(k, far, len(NEAR)).start()

        count_copies[heads + k].start()
    for k in range(heads):
        head_copies[k].start()
        count_copies[k].start()

    def tile_of(k):
        return tiles[k].reshape(block, width)

    def scores_of(rounded, tile):
        return lax.dot_general(rounded, tile, (((1,), (1,)), ((), ())), preferred_element_type=jnp.float32)

    def dense_part(vector):
        return jnp.dot(vector, gram[...], precision=lax.Precision.HIGHEST, preferred_element_type=jnp.float32) + ridge_term * vector

    def apply_operator(vector):
        rounded = vector.astype(jnp.bfloat16)
        acc[...] = dense_part(vector)

        def some_tiles(i, carry):
            part = None
            for j in range(4):
                k = i * 4 + j
                tile = tile_of(k)
                scaled = (scores_of(rounded, tile) * weights[k]).astype(jnp.bfloat16)
                data = jnp.dot(scaled, tile, preferred_element_type=jnp.float32)
                part = data if part is None else part + data
            acc[...] += part
            return carry

        lax.fori_loop(0, total // 4, some_tiles, 0)
        return acc[...]

    solution = start[...]
    rounded = solution.astype(jnp.bfloat16)
    for copy in gram_copies:
        copy.wait()
    gram[...] = (halves[0].astype(jnp.float32) + halves[1].astype(jnp.float32)).reshape(width, width)
    acc[...] = -dense_part(solution)

    def first_tiles(first, i):
        part = None
        for j in range(2):
            k = first + i * 2 + j
            tile = tile_of(k)
            count = counts[k].astype(jnp.float32)
            weight = conf_alpha * count
            weights[k] = weight
            rated = jnp.where(count > 0.0, 1.0 + weight, 0.0).astype(jnp.bfloat16)
            scaled = (scores_of(rounded, tile) * weight).astype(jnp.bfloat16)
            data = jnp.dot(rated, tile, preferred_element_type=jnp.float32) - jnp.dot(
                scaled, tile, preferred_element_type=jnp.float32
            )
            part = data if part is None else part + data
        acc[...] += part

    def count_wait(k):
        pltpu.make_async_copy(head_counts.at[0, 0], counts.at[k], count_sems.at[k]).wait()

    def first_tails(i, carry):
        for j in range(2):
            k = i * 2 + j
            tail_copy(k, near, 0, True).wait()
            count_wait(heads + k)
        first_tiles(heads, i)
        return carry

    def first_heads(i, carry):
        for j in range(2):
            count_wait(i * 2 + j)
        first_tiles(0, i)
        return carry

    lax.fori_loop(0, tails // 2, first_tails, 0)
    for copy in head_copies:
        copy.wait()
    lax.fori_loop(0, heads // 2, first_heads, 0)
    residual = acc[...]
    direction = residual
    norm_now = jnp.sum(residual * residual, axis=1, keepdims=True)
    for turn_index in range(ITERS):
        image = apply_operator(direction)
        step_size = norm_now / (jnp.sum(direction * image, axis=1, keepdims=True) + epsilon)
        solution = solution + step_size * direction
        residual = residual - step_size * image
        if turn_index + 1 < ITERS:
            norm_next = jnp.sum(residual * residual, axis=1, keepdims=True)
            direction = residual + norm_next / (norm_now + epsilon) * direction
            norm_now = norm_next
    new_out[...] = solution
    res_out[...] = residual


def solve(slab, slot, user, start, near, far, same, other, head_counts, tail_counts):
    block, width = start.shape
    band = same.shape[2]
    total = head_counts.shape[1] + tail_counts.shape[1]
    out = jax.ShapeDtypeStruct((block, width), jnp.float32)
    return pl.pallas_call(
        solve_kernel,
        name="solve",
        grid_spec=pltpu.PrefetchScalarGridSpec(
            num_scalar_prefetch=3,
            grid=(1,),
            in_specs=[whole(start)] + [pl.BlockSpec(memory_space=pl.ANY)] * 6,
            out_specs=(whole(start), whole(start)),
            scratch_shapes=[
                pltpu.VMEM((total, USER, band, width), jnp.bfloat16),
                pltpu.VMEM((total, block, block), jnp.float32),
                pltpu.VMEM((total, block, block), jnp.int32),
                pltpu.VMEM((2, USER, width // USER, width), jnp.bfloat16),
                pltpu.VMEM((width, width), jnp.float32),
                pltpu.VMEM((block, width), jnp.float32),
                pltpu.SemaphoreType.DMA((total,)),
                pltpu.SemaphoreType.DMA((total,)),
                pltpu.SemaphoreType.DMA((USER,)),
                pltpu.SemaphoreType.DMA((USER,)),
            ],
        ),
        out_shape=(out, out),
    )(slab, slot, user.reshape(1), start, near, far, same, other, head_counts, tail_counts)


def ring(step, size=Z_SIZE):
    return [(i, (i + step) % size) for i in range(size)]


def line(step):
    return [(i, (i + 2 * step) % USER) for i in range(USER)]


def local(user_factors, item_factors, head_ids, tail_ids, head_counts, tail_counts):
    user, y, z = (lax.axis_index(axis) for axis in ALL)
    block_size = head_counts.shape[-1]
    width = item_factors.shape[1]
    per_shard = item_factors.shape[0] // block_size

    own = prepare(item_factors.reshape(per_shard, block_size, width), user)

    ids = tail_ids.reshape(-1)
    owner_of, local_of = ids // per_shard, ids % per_shard
    owners = jnp.arange(Y_SIZE * Z_SIZE, dtype=jnp.int32)
    requests = jnp.sum(jnp.where(owner_of[:, None] == owners[None, :], local_of[:, None], 0), axis=0)
    requests = jnp.tile(requests.reshape(Y_SIZE, Z_SIZE), (USER, 1))
    wanted = lax.all_to_all(requests, PLANE, 0, 0, tiled=True)

    up = down = own
    pieces = [own]
    near = None
    for turn in range(1, 4):
        up = lax.ppermute(up, "z", ring(1))
        down = lax.ppermute(down, "z", ring(-1))
        pieces += [up, down]
        if turn == 1:
            served_near = pick_near(wanted, z, pieces)
            near = lax.all_to_all(served_near, PLANE, 0, 0, tiled=True)
    pieces.append(lax.ppermute(up, "z", ring(1)))
    served_far, shared = pick_far(wanted, head_ids, z, pieces)
    far = lax.all_to_all(served_far, PLANE, 0, 0, tiled=True)
    slabs = [shared] + [lax.ppermute(shared, "y", ring(-step, Y_SIZE)) for step in range(1, Y_SIZE)]
    merged = merge(head_ids // (per_shard * Z_SIZE), y, slabs)
    same = jnp.stack([merged] + [lax.ppermute(merged, "user", line(-step)) for step in range(1, USER // 2)])
    other = lax.ppermute(same, "user", [(i, i ^ 1) for i in range(USER)])

    slot = jnp.asarray(SLOT_OF_SHIFT, jnp.int32)[(owner_of - z) % Z_SIZE]
    near = near.reshape(USER, Y_SIZE, *near.shape[1:])
    far = far.reshape(USER, Y_SIZE, *far.shape[1:])
    return solve(owner_of // Z_SIZE, slot, user, user_factors, near, far, same, other, head_counts, tail_counts)


def solution(mesh):
    fine = Mesh(mesh.devices.reshape(USER, Y_SIZE, Z_SIZE), ALL)
    return jax.shard_map(
        local,
        mesh=fine,
        in_specs=(P(ALL, None), P(("y", "z"), None), P(), P(ALL, None), P(ALL, None, None, None), P(ALL, None, None, None)),
        out_specs=(P(ALL, None), P(ALL, None)),
        check_vma=False,
    )
```

time: 1520 us -> 158 us (0.10)
  waiting for transfers between devices: 1370 us -> 69.3 us
  starting transfers between devices: 5.04 us -> 42 us
  Pallas kernels: 0 us -> 35.3 us
  local copies, waits for them, and re-layouts: 41.4 us -> 6.7 us
  matrix products: 30.6 us -> 0 us
  blocking collectives: 21.1 us -> 0 us
  loops' own time: 20.3 us -> 0 us
    psum x9 -> x0, waiting for transfers between devices: 1370 us -> none  [the longest x8 1140 us: broadcast(): return lax.psum(jnp.where(mine, shard, jnp.zeros_like(shard)), axis)]
    ppermute x0 -> x14, waiting for transfers between devices: none -> 63.2 us  [the longest x3 33.8 us: local(): lax.ppermute(shared, 'y', ring(-step, Y_SIZE))]
    pallas_call x0 -> x5, Pallas kernels: none -> 35.3 us  [the longest x1 21.4 us: solve(): pl.pallas_call(solve_kernel, name='solve', grid_spec=pltpu.PrefetchScalar...]
    dot_general x8 -> x0, matrix products: 30.6 us -> none  [the longest x3 21.3 us: apply_operator(): jnp.einsum('kui,kif->uf', scaled, item_tiles, preferred_element_type=jnp....]
    ppermute x0 -> x14, starting transfers between devices: none -> 21.7 us  [the longest x3 10.4 us: local(): down = lax.ppermute(down, 'z', ring(-1))]
    all_to_all x1 -> x0, blocking collectives: 21.1 us -> none  [local(): lax.all_to_all(requests, 'item', split_axis=0, concat_axis=0, tiled=True)]
    another operation x1 -> x0, loops' own time: 20.3 us -> none  [local(): head_rows = lax.fori_loop(0, head_total, take_turn, empty)]
    all_to_all x1 -> x3, starting transfers between devices: 4.98 us -> 20.3 us  [the longest x1 7.62 us: local(): wanted = lax.all_to_all(requests, PLANE, 0, 0, tiled=True)]
  transfers between devices with their start and end apart: 10 -> 17, of which waited for: 9 -> 11; matrix products, arithmetic and copies ran while one was open for 4% -> 3% of each run, Pallas kernels for 0% -> 5%
where the time goes in v1:
time: 158 us; the launch traced here: 157 us
  waiting for transfers between devices  69.3 us (44%)
  starting transfers between devices  42 us (27%)
  Pallas kernels  35.3 us (22%)
  local copies, waits for them, and re-layouts  6.7 us (4%)
  other arithmetic  2.23 us (1%)
    ppermute x3, waiting for transfers between devices, local(): lax.ppermute(shared, 'y', ring(-step, Y_SIZE))  33.8 us
    pallas_call x1, Pallas kernels, solve(): pl.pallas_call(solve_kernel, name='solve', grid_spec=pltpu.PrefetchScalar...  21.4 us
    ppermute x3, waiting for transfers between devices, local(): up = lax.ppermute(up, 'z', ring(1))  13.2 us
    ppermute x3, starting transfers between devices, local(): down = lax.ppermute(down, 'z', ring(-1))  10.4 us
    ppermute x1, waiting for transfers between devices, local(): pieces.append(lax.ppermute(up, 'z', ring(1)))  8.54 us
    all_to_all x1, starting transfers between devices, local(): wanted = lax.all_to_all(requests, PLANE, 0, 0, tiled=True)  7.62 us
    all_to_all x1, starting transfers between devices, local(): far = lax.all_to_all(served_far, PLANE, 0, 0, tiled=True)  7.44 us
    ppermute x3, waiting for transfers between devices, local(): lax.ppermute(merged, 'user', line(-step))  6.65 us
  transfers between devices with their start and end apart: 17, of which 11 were waited for; matrix products, arithmetic and copies ran while one was open for 3% of the time, Pallas kernels for 5%

profile of v1, /device:TPU:2, one launch (start us, length us, event | category | flops | bytes accessed | tf_op | source)
XLA Modules:
  0.0 156.5 jit_solution(18173719422054729696)
XLA Ops:
  0.6 3.1 %prepare.1.own.refs_0_ = bf16[18,32,256]{2,1,0:T(8,128)(2,1)} custom-call(s32[1]{0:T(128)} %bitcast.3.place, bf16[16,256,256]{2,1,0:T(8,128)(2,1)} %bitcast.42), custom_call_target="tpu_custom_call" | custom-call | tf_op jit(solution)/shard_map/prepare/pallas_call | solution.py:54
  3.7 1.9 %collective-permute-start = (bf16[18,32,256]{2,1,0:T(8,128)(2,1)}, bf16[18,32,256]{2,1,0:T(8,128)(2,1)S(1)}, u32[]{:S(2)}, u32[]{:S(2)}) collective-permute-start(bf16[18,32,256]{2,1,0:T(8,128)(2,1)} %prepare.1.own.refs_0_), channel_id=1, source_target_pairs={{0,1},{1,2},{2,3},{3,4},{4,5},{5,6},{6,7},{7,0},{8,9},{9,10},{10,1... | collective-permute-start | bytes 884744 | tf_op jit(solution)/shard_map/ppermute | solution.py:364
  5.6 3.9 %collective-permute-start.1 = (bf16[18,32,256]{2,1,0:T(8,128)(2,1)}, bf16[18,32,256]{2,1,0:T(8,128)(2,1)S(1)}, u32[]{:S(2)}, u32[]{:S(2)}) collective-permute-start(bf16[18,32,256]{2,1,0:T(8,128)(2,1)} %prepare.1.own.refs_0_), channel_id=1, source_target_pairs={{0,7},{1,0},{2,1},{3,2},{4,3},{5,4},{6,5},{7,6},{8,15},{9,8},{10,9... | collective-permute-start | bytes 884744 | tf_op jit(solution)/shard_map/ppermute | solution.py:365
  10.9 7.6 %all-to-all-start = ((s32[32,1,8]{2,1,0:T(1,128)}), s32[32,1,8]{2,1,0:T(1,128)S(1)}, u32[]{:S(2)}, u32[]{:S(2)}) async-start(s32[32,1,8]{2,1,0:T(1,128)} %bitcast.4), calls=%async_computation | async-start | bytes 32768 | tf_op jit(solution)/shard_map/all_to_all | solution.py:358
  18.6 6.1 %all-to-all-done = s32[32,1,8]{2,1,0:T(1,128)S(1)} async-done(((s32[32,1,8]{2,1,0:T(1,128)}), s32[32,1,8]{2,1,0:T(1,128)S(1)}, u32[]{:S(2)}, u32[]{:S(2)}) %all-to-all-start) | async-done | bytes 1056 | tf_op jit(solution)/shard_map/all_to_all | solution.py:358
  25.5 3.3 %pick_near.1 = bf16[32,96,256]{2,1,0:T(8,128)(2,1)} custom-call(s32[32,8]{1,0:T(8,128)} %bitcast.47, s32[1]{0:T(128)} %bitcast.6.place, bf16[18,32,256]{2,1,0:T(8,128)(2,1)} %prepare.1.own.refs_0_, bf16[18,32,256]{2,1,0:T(8,128)(2,1)} %copy-done.4, bf16[18,32,256]{2,1,0:T(8,128)(2,1)} %copy-done.6), custom_call_target="tpu_custom_call" | custom-call | tf_op jit(solution)/shard_map/pick_near/pallas_call | solution.py:81
  28.8 5.2 %all-to-all-start.1 = ((bf16[32,96,256]{2,1,0:T(8,128)(2,1)}), bf16[32,96,256]{2,1,0:T(8,128)(2,1)S(1)}, u32[]{:S(2)}, u32[]{:S(2)}) async-start(bf16[32,96,256]{2,1,0:T(8,128)(2,1)} %pick_near.1), calls=%async_computation.1 | async-start | bytes 3145728 | tf_op jit(solution)/shard_map/all_to_all | solution.py:369
  34.2 3.2 %collective-permute-start.3 = (bf16[18,32,256]{2,1,0:T(8,128)(2,1)S(1)}, bf16[18,32,256]{2,1,0:T(8,128)(2,1)S(1)}, u32[]{:S(2)}, u32[]{:S(2)}) collective-permute-start(bf16[18,32,256]{2,1,0:T(8,128)(2,1)S(1)} %copy-done.7), channel_id=1, source_target_pairs={{0,7},{1,0},{2,1},{3,2},{4,3},{5,4},{6,5},{7,6},{8,15},{9,8},{10,9... | collective-permute-start | bytes 884744 | tf_op jit(solution)/shard_map/ppermute | solution.py:365
  37.4 7.0 %collective-permute-done.2.refs_3_ = bf16[18,32,256]{2,1,0:T(8,128)(2,1)S(1)} collective-permute-done((bf16[18,32,256]{2,1,0:T(8,128)(2,1)S(1)}, bf16[18,32,256]{2,1,0:T(8,128)(2,1)S(1)}, u32[]{:S(2)}, u32[]{:S(2)}) %collective-permute-start.2) | collective-permute-done | bytes 294944 | tf_op jit(solution)/shard_map/ppermute | solution.py:364
  44.4 3.2 %collective-permute-start.5 = (bf16[18,32,256]{2,1,0:T(8,128)(2,1)S(1)}, bf16[18,32,256]{2,1,0:T(8,128)(2,1)S(1)}, u32[]{:S(2)}, u32[]{:S(2)}) collective-permute-start(bf16[18,32,256]{2,1,0:T(8,128)(2,1)S(1)} %collective-permute-done.3.refs_4_), channel_id=1, source_target_pairs={{0,7},{1,0},{2,1},{3,2},{4,3},{5,4},{6,5},{7,6},{8,15},{9,8},{10,9... | collective-permute-start | bytes 884744 | tf_op jit(solution)/shard_map/ppermute | solution.py:365
  47.7 6.2 %collective-permute-done.4.refs_5_ = bf16[18,32,256]{2,1,0:T(8,128)(2,1)S(1)} collective-permute-done((bf16[18,32,256]{2,1,0:T(8,128)(2,1)S(1)}, bf16[18,32,256]{2,1,0:T(8,128)(2,1)S(1)}, u32[]{:S(2)}, u32[]{:S(2)}) %collective-permute-start.4) | collective-permute-done | bytes 294944 | tf_op jit(solution)/shard_map/ppermute | solution.py:364
  53.8 8.5 %collective-permute-done.6.refs_7_ = bf16[18,32,256]{2,1,0:T(8,128)(2,1)S(1)} collective-permute-done((bf16[18,32,256]{2,1,0:T(8,128)(2,1)S(1)}, bf16[18,32,256]{2,1,0:T(8,128)(2,1)S(1)}, u32[]{:S(2)}, u32[]{:S(2)}) %collective-permute-start.6) | collective-permute-done | bytes 294944 | tf_op jit(solution)/shard_map/ppermute | solution.py:370
  63.1 4.9 %pick_far.1 = (bf16[32,160,256]{2,1,0:T(8,128)(2,1)}, bf16[10,32,256]{2,1,0:T(8,128)(2,1)}) custom-call(s32[32,8]{1,0:T(8,128)} %bitcast.48, s32[8]{0:T(128)} %head_ids.1, s32[1]{0:T(128)} %bitcast.6.place, bf16[18,32,256]{2,1,0:T(8,128)(2,1)} %prepare.1.own.refs_0_, bf16[18,32,256]{2,1,0:T(8,128)(2,1)} %copy-done.4, bf16[18,32,256]{2,1,0:T(8,128)(2,1)} %copy-done.6, ...), custom_call_target="tpu_custom_call" | custom-call | tf_op jit(solution)/shard_map/pick_far/pallas_call | solution.py:131
  69.1 7.4 %all-to-all-start.2 = ((bf16[32,160,256]{2,1,0:T(8,128)(2,1)}), bf16[32,160,256]{2,1,0:T(8,128)(2,1)S(1)}, u32[]{:S(2)}, u32[]{:S(2)}) async-start(bf16[32,160,256]{2,1,0:T(8,128)(2,1)} %get-tuple-element.4), calls=%async_computation.2 | async-start | bytes 5242880 | tf_op jit(solution)/shard_map/all_to_all | solution.py:372
  76.6 2.8 %collective-permute-start.7 = (bf16[10,32,256]{2,1,0:T(8,128)(2,1)S(1)}, bf16[10,32,256]{2,1,0:T(8,128)(2,1)S(1)}, u32[]{:S(2)}, u32[]{:S(2)}) collective-permute-start(bf16[10,32,256]{2,1,0:T(8,128)(2,1)S(1)} %copy-done.13), channel_id=1, source_target_pairs={{0,24},{8,0},{16,8},{24,16},{1,25},{9,1},{17,9},{25,17},{2,26},{10... | collective-permute-start | bytes 491528 | tf_op jit(solution)/shard_map/ppermute | solution.py:373
  81.6 29.8 %collective-permute-done.7.above = bf16[10,32,256]{2,1,0:T(8,128)(2,1)S(1)} collective-permute-done((bf16[10,32,256]{2,1,0:T(8,128)(2,1)S(1)}, bf16[10,32,256]{2,1,0:T(8,128)(2,1)S(1)}, u32[]{:S(2)}, u32[]{:S(2)}) %collective-permute-start.7) | collective-permute-done | bytes 163872 | tf_op jit(solution)/shard_map/ppermute | solution.py:373
  111.4 2.1 %collective-permute-done.8.across = bf16[10,32,256]{2,1,0:T(8,128)(2,1)S(1)} collective-permute-done((bf16[10,32,256]{2,1,0:T(8,128)(2,1)S(1)}, bf16[10,32,256]{2,1,0:T(8,128)(2,1)S(1)}, u32[]{:S(2)}, u32[]{:S(2)}) %collective-permute-start.8) | collective-permute-done | bytes 163872 | tf_op jit(solution)/shard_map/ppermute | solution.py:373
  113.5 2.0 %collective-permute-done.9.below = bf16[10,32,256]{2,1,0:T(8,128)(2,1)S(1)} collective-permute-done((bf16[10,32,256]{2,1,0:T(8,128)(2,1)S(1)}, bf16[10,32,256]{2,1,0:T(8,128)(2,1)S(1)}, u32[]{:S(2)}, u32[]{:S(2)}) %collective-permute-start.9) | collective-permute-done | bytes 163872 | tf_op jit(solution)/shard_map/ppermute | solution.py:373
  116.1 2.6 %merge.1 = bf16[10,32,256]{2,1,0:T(8,128)(2,1)} custom-call(s32[8]{0:T(128)} %and_select_fusion.slabs, s32[1]{0:T(128)} %bitcast.10.place, bf16[10,32,256]{2,1,0:T(8,128)(2,1)} %get-tuple-element.5.own, bf16[10,32,256]{2,1,0:T(8,128)(2,1)} %copy-done.14, bf16[10,32,256]{2,1,0:T(8,128)(2,1)} %copy-done.15, bf16[10,32,256]{2,1,0:T(8,128)(2,1)} %copy-done.16), custom_call_target="tpu_custom_call" | custom-call | tf_op jit(solution)/shard_map/merge/pallas_call | solution.py:165
  118.7 1.5 collective-permute-start.12
  121.3 2.2 %collective-permute-start.10 = (bf16[10,32,256]{2,1,0:T(8,128)(2,1)}, bf16[10,32,256]{2,1,0:T(8,128)(2,1)S(1)}, u32[]{:S(2)}, u32[]{:S(2)}) collective-permute-start(bf16[10,32,256]{2,1,0:T(8,128)(2,1)} %merge.1), channel_id=1, source_target_pairs={{0,192},{32,224},{64,0},{96,32},{128,64},{160,96},{192,128},{224,1... | collective-permute-start | bytes 491528 | tf_op jit(solution)/shard_map/ppermute | solution.py:375
  123.4 2.1 %collective-permute-done.12 = bf16[10,32,256]{2,1,0:T(8,128)(2,1)S(1)} collective-permute-done((bf16[10,32,256]{2,1,0:T(8,128)(2,1)}, bf16[10,32,256]{2,1,0:T(8,128)(2,1)S(1)}, u32[]{:S(2)}, u32[]{:S(2)}) %collective-permute-start.12) | collective-permute-done | bytes 163872 | tf_op jit(solution)/shard_map/ppermute | solution.py:375
  125.5 3.4 %collective-permute-done.11 = bf16[10,32,256]{2,1,0:T(8,128)(2,1)S(1)} collective-permute-done((bf16[10,32,256]{2,1,0:T(8,128)(2,1)}, bf16[10,32,256]{2,1,0:T(8,128)(2,1)S(1)}, u32[]{:S(2)}, u32[]{:S(2)}) %collective-permute-start.11) | collective-permute-done | bytes 163872 | tf_op jit(solution)/shard_map/ppermute | solution.py:375
  134.9 21.4 %solve.1 = (f32[256,256]{1,0:T(8,128)}, f32[256,256]{1,0:T(8,128)}) custom-call(s32[16]{0:T(128)} %get-tuple-element.6.slab, s32[16]{0:T(128)} %gather_fusion, s32[1]{0:T(128)} %bitcast.3.place, f32[256,256]{1,0:T(8,128)} %start.1, bf16[8,4,96,256]{3,2,1,0:T(8,128)(2,1)} %bitcast.41, bf16[8,4,160,256]{3,2,1,0:T(8,128)(2,1)} %bitcast.40, ...), custom_call_target="tpu_custom_call" | custom-call | tf_op jit(solution)/shard_map/solve/pallas_call | solution.py:312
  (64 shorter events, 14.1 us)
Async XLA Ops:
  0.6 8.9 %copy-start.19 = (s32[1,16]{1,0:T(1,128)S(1)}, s32[1,16]{1,0:T(1,128)}, u32[]{:S(2)}) copy-start(s32[1,16]{1,0:T(1,128)} %param.10) | copy-start | bytes 196
  3.7 21.0 %collective-permute-start = (bf16[18,32,256]{2,1,0:T(8,128)(2,1)}, bf16[18,32,256]{2,1,0:T(8,128)(2,1)S(1)}, u32[]{:S(2)}, u32[]{:S(2)}) collective-permute-start(bf16[18,32,256]{2,1,0:T(8,128)(2,1)} %prepare.1.own.refs_0_), channel_id=1, source_target_pairs={{0,1},{1,2},{2,3},{3,4},{4,5},{5,6},{6,7},{7,0},{8,9},{9,10},{10,1... | collective-permute-start | bytes 884744 | tf_op jit(solution)/shard_map/ppermute | solution.py:364
  5.6 19.1 %collective-permute-start.1 = (bf16[18,32,256]{2,1,0:T(8,128)(2,1)}, bf16[18,32,256]{2,1,0:T(8,128)(2,1)S(1)}, u32[]{:S(2)}, u32[]{:S(2)}) collective-permute-start(bf16[18,32,256]{2,1,0:T(8,128)(2,1)} %prepare.1.own.refs_0_), channel_id=1, source_target_pairs={{0,7},{1,0},{2,1},{3,2},{4,3},{5,4},{6,5},{7,6},{8,15},{9,8},{10,9... | collective-permute-start | bytes 884744 | tf_op jit(solution)/shard_map/ppermute | solution.py:365
  10.9 13.7 %all-to-all-start = ((s32[32,1,8]{2,1,0:T(1,128)}), s32[32,1,8]{2,1,0:T(1,128)S(1)}, u32[]{:S(2)}, u32[]{:S(2)}) async-start(s32[32,1,8]{2,1,0:T(1,128)} %bitcast.4), calls=%async_computation | async-start | bytes 32768 | tf_op jit(solution)/shard_map/all_to_all | solution.py:358
  28.8 39.1 %all-to-all-start.1 = ((bf16[32,96,256]{2,1,0:T(8,128)(2,1)}), bf16[32,96,256]{2,1,0:T(8,128)(2,1)S(1)}, u32[]{:S(2)}, u32[]{:S(2)}) async-start(bf16[32,96,256]{2,1,0:T(8,128)(2,1)} %pick_near.1), calls=%async_computation.1 | async-start | bytes 3145728 | tf_op jit(solution)/shard_map/all_to_all | solution.py:369
  34.1 10.3 %collective-permute-start.2 = (bf16[18,32,256]{2,1,0:T(8,128)(2,1)S(1)}, bf16[18,32,256]{2,1,0:T(8,128)(2,1)S(1)}, u32[]{:S(2)}, u32[]{:S(2)}) collective-permute-start(bf16[18,32,256]{2,1,0:T(8,128)(2,1)S(1)} %copy-done.5), channel_id=1, source_target_pairs={{0,1},{1,2},{2,3},{3,4},{4,5},{5,6},{6,7},{7,0},{8,9},{9,10},{10,1... | collective-permute-start | bytes 884744 | tf_op jit(solution)/shard_map/ppermute | solution.py:364
  34.2 10.3 %collective-permute-start.3 = (bf16[18,32,256]{2,1,0:T(8,128)(2,1)S(1)}, bf16[18,32,256]{2,1,0:T(8,128)(2,1)S(1)}, u32[]{:S(2)}, u32[]{:S(2)}) collective-permute-start(bf16[18,32,256]{2,1,0:T(8,128)(2,1)S(1)} %copy-done.7), channel_id=1, source_target_pairs={{0,7},{1,0},{2,1},{3,2},{4,3},{5,4},{6,5},{7,6},{8,15},{9,8},{10,9... | collective-permute-start | bytes 884744 | tf_op jit(solution)/shard_map/ppermute | solution.py:365
  44.4 18.0 %copy-start.8 = (bf16[18,32,256]{2,1,0:T(8,128)(2,1)}, bf16[18,32,256]{2,1,0:T(8,128)(2,1)S(1)}, u32[]{:S(2)}) copy-start(bf16[18,32,256]{2,1,0:T(8,128)(2,1)S(1)} %collective-permute-done.2.refs_3_) | copy-start | bytes 884740
  44.4 9.4 %collective-permute-start.4 = (bf16[18,32,256]{2,1,0:T(8,128)(2,1)S(1)}, bf16[18,32,256]{2,1,0:T(8,128)(2,1)S(1)}, u32[]{:S(2)}, u32[]{:S(2)}) collective-permute-start(bf16[18,32,256]{2,1,0:T(8,128)(2,1)S(1)} %collective-permute-done.2.refs_3_), channel_id=1, source_target_pairs={{0,1},{1,2},{2,3},{3,4},{4,5},{5,6},{6,7},{7,0},{8,9},{9,10},{10,1... | collective-permute-start | bytes 884744 | tf_op jit(solution)/shard_map/ppermute | solution.py:364
  44.4 18.0 %copy-start.9 = (bf16[18,32,256]{2,1,0:T(8,128)(2,1)}, bf16[18,32,256]{2,1,0:T(8,128)(2,1)S(1)}, u32[]{:S(2)}) copy-start(bf16[18,32,256]{2,1,0:T(8,128)(2,1)S(1)} %collective-permute-done.3.refs_4_) | copy-start | bytes 884740
  44.4 9.4 %collective-permute-start.5 = (bf16[18,32,256]{2,1,0:T(8,128)(2,1)S(1)}, bf16[18,32,256]{2,1,0:T(8,128)(2,1)S(1)}, u32[]{:S(2)}, u32[]{:S(2)}) collective-permute-start(bf16[18,32,256]{2,1,0:T(8,128)(2,1)S(1)} %collective-permute-done.3.refs_4_), channel_id=1, source_target_pairs={{0,7},{1,0},{2,1},{3,2},{4,3},{5,4},{6,5},{7,6},{8,15},{9,8},{10,9... | collective-permute-start | bytes 884744 | tf_op jit(solution)/shard_map/ppermute | solution.py:365
  53.8 8.6 %copy-start.10 = (bf16[18,32,256]{2,1,0:T(8,128)(2,1)}, bf16[18,32,256]{2,1,0:T(8,128)(2,1)S(1)}, u32[]{:S(2)}) copy-start(bf16[18,32,256]{2,1,0:T(8,128)(2,1)S(1)} %collective-permute-done.4.refs_5_) | copy-start | bytes 884740
  53.8 8.6 %collective-permute-start.6 = (bf16[18,32,256]{2,1,0:T(8,128)(2,1)S(1)}, bf16[18,32,256]{2,1,0:T(8,128)(2,1)S(1)}, u32[]{:S(2)}, u32[]{:S(2)}) collective-permute-start(bf16[18,32,256]{2,1,0:T(8,128)(2,1)S(1)} %collective-permute-done.4.refs_5_), channel_id=1, source_target_pairs={{0,1},{1,2},{2,3},{3,4},{4,5},{5,6},{6,7},{7,0},{8,9},{9,10},{10,1... | collective-permute-start | bytes 884744 | tf_op jit(solution)/shard_map/ppermute | solution.py:370
  68.0 8.6 %copy-start.13 = (bf16[10,32,256]{2,1,0:T(8,128)(2,1)S(1)}, bf16[10,32,256]{2,1,0:T(8,128)(2,1)}, u32[]{:S(2)}) copy-start(bf16[10,32,256]{2,1,0:T(8,128)(2,1)} %get-tuple-element.5.own) | copy-start | bytes 491524
  68.0 13.1 %copy-start.18 = (s32[8]{0:T(128)S(1)}, s32[8]{0:T(128)}, u32[]{:S(2)}) copy-start(s32[8]{0:T(128)} %head_ids.1) | copy-start | bytes 100
  69.1 64.3 %all-to-all-start.2 = ((bf16[32,160,256]{2,1,0:T(8,128)(2,1)}), bf16[32,160,256]{2,1,0:T(8,128)(2,1)S(1)}, u32[]{:S(2)}, u32[]{:S(2)}) async-start(bf16[32,160,256]{2,1,0:T(8,128)(2,1)} %get-tuple-element.4), calls=%async_computation.2 | async-start | bytes 5242880 | tf_op jit(solution)/shard_map/all_to_all | solution.py:372
  76.6 54.7 %copy-start = (s32[8]{0:T(128)S(1)}, s32[8]{0:T(128)}, u32[]{:S(2)}) copy-start(s32[8]{0:T(128)} %constant.77.clone) | copy-start | bytes 100
  76.6 34.7 %collective-permute-start.7 = (bf16[10,32,256]{2,1,0:T(8,128)(2,1)S(1)}, bf16[10,32,256]{2,1,0:T(8,128)(2,1)S(1)}, u32[]{:S(2)}, u32[]{:S(2)}) collective-permute-start(bf16[10,32,256]{2,1,0:T(8,128)(2,1)S(1)} %copy-done.13), channel_id=1, source_target_pairs={{0,24},{8,0},{16,8},{24,16},{1,25},{9,1},{17,9},{25,17},{2,26},{10... | collective-permute-start | bytes 491528 | tf_op jit(solution)/shard_map/ppermute | solution.py:373
  79.4 34.1 %collective-permute-start.8 = (bf16[10,32,256]{2,1,0:T(8,128)(2,1)S(1)}, bf16[10,32,256]{2,1,0:T(8,128)(2,1)S(1)}, u32[]{:S(2)}, u32[]{:S(2)}) collective-permute-start(bf16[10,32,256]{2,1,0:T(8,128)(2,1)S(1)} %copy-done.13), channel_id=1, source_target_pairs={{0,16},{8,24},{16,0},{24,8},{1,17},{9,25},{17,1},{25,9},{2,18},{10... | collective-permute-start | bytes 491528 | tf_op jit(solution)/shard_map/ppermute | solution.py:373
  80.2 35.2 %collective-permute-start.9 = (bf16[10,32,256]{2,1,0:T(8,128)(2,1)S(1)}, bf16[10,32,256]{2,1,0:T(8,128)(2,1)S(1)}, u32[]{:S(2)}, u32[]{:S(2)}) collective-permute-start(bf16[10,32,256]{2,1,0:T(8,128)(2,1)S(1)} %copy-done.13), channel_id=1, source_target_pairs={{0,8},{8,16},{16,24},{24,0},{1,9},{9,17},{17,25},{25,1},{2,10},{10... | collective-permute-start | bytes 491528 | tf_op jit(solution)/shard_map/ppermute | solution.py:373
  118.7 6.9 %collective-permute-start.12 = (bf16[10,32,256]{2,1,0:T(8,128)(2,1)}, bf16[10,32,256]{2,1,0:T(8,128)(2,1)S(1)}, u32[]{:S(2)}, u32[]{:S(2)}) collective-permute-start(bf16[10,32,256]{2,1,0:T(8,128)(2,1)} %merge.1), channel_id=1, source_target_pairs={{0,64},{32,96},{64,128},{96,160},{128,192},{160,224},{192,0},{224,... | collective-permute-start | bytes 491528 | tf_op jit(solution)/shard_map/ppermute | solution.py:375
  120.2 8.8 %collective-permute-start.11 = (bf16[10,32,256]{2,1,0:T(8,128)(2,1)}, bf16[10,32,256]{2,1,0:T(8,128)(2,1)S(1)}, u32[]{:S(2)}, u32[]{:S(2)}) collective-permute-start(bf16[10,32,256]{2,1,0:T(8,128)(2,1)} %merge.1), channel_id=1, source_target_pairs={{0,128},{32,160},{64,192},{96,224},{128,0},{160,32},{192,64},{224,... | collective-permute-start | bytes 491528 | tf_op jit(solution)/shard_map/ppermute | solution.py:375
  121.3 8.8 %collective-permute-start.10 = (bf16[10,32,256]{2,1,0:T(8,128)(2,1)}, bf16[10,32,256]{2,1,0:T(8,128)(2,1)S(1)}, u32[]{:S(2)}, u32[]{:S(2)}) collective-permute-start(bf16[10,32,256]{2,1,0:T(8,128)(2,1)} %merge.1), channel_id=1, source_target_pairs={{0,192},{32,224},{64,0},{96,32},{128,64},{160,96},{192,128},{224,1... | collective-permute-start | bytes 491528 | tf_op jit(solution)/shard_map/ppermute | solution.py:375
  131.1 2.3 %collective-permute-start.13 = (bf16[4,10,32,256]{3,2,1,0:T(8,128)(2,1)S(1)}, bf16[4,10,32,256]{3,2,1,0:T(8,128)(2,1)}, u32[]{:S(2)}, u32[]{:S(2)}) collective-permute-start(bf16[4,10,32,256]{3,2,1,0:T(8,128)(2,1)S(1)} %pad_maximum_fusion.same), channel_id=1, source_target_pairs={{0,32},{32,0},{64,96},{96,64},{128,160},{160,128},{192,224},{224,1... | collective-permute-start | bytes 1966088 | tf_op jit(solution)/shard_map/ppermute | solution.py:376
  (13 other events, 33.7 us)

commit v2 on v1

v2 whole, which is shorter than its diff:
```python
import functools

import jax
import jax.numpy as jnp
from jax import lax
from jax.experimental import pallas as pl
from jax.experimental.pallas import tpu as pltpu
from jax.sharding import Mesh, PartitionSpec as P

ITERS = 2

conf_alpha = 4.0
ridge_term = 0.1
epsilon = 1e-06

USER, Y_SIZE, Z_SIZE = 8, 4, 8
ALL = ("user", "y", "z")
PLANE = ("user", "y")
PARTS = ((0, -1, 1), (-2, 2), (-3, 3, 4))
OFFSETS = sum(PARTS, ())
FIRST = tuple(sum(len(part) for part in PARTS[:n]) for n in range(len(PARTS)))
SLOT_OF_SHIFT = tuple(OFFSETS.index(s if s <= 4 else s - 8) for s in range(8))


MIB = 1 << 20
IN_VMEM = pl.BlockSpec(memory_space=pltpu.VMEM)


def limit(mib):
    return pltpu.CompilerParams(vmem_limit_bytes=mib * MIB)


def bf16(*shape):
    return jax.ShapeDtypeStruct(shape, jnp.bfloat16)


def store_split(out, at, values):
    high = values.astype(jnp.bfloat16)
    out[at] = high
    out[at + 1] = (values - high.astype(jnp.float32)).astype(jnp.bfloat16)


def prepare_kernel(place, blocks, out, gram):
    total, block, width = blocks.shape
    band = block // USER
    row = pl.multiple_of(place[0] * band, band)
    for k in range(total):
        rows = blocks[k]
        part = lax.dot_general(rows, rows, (((0,), (0,)), ((), ())), preferred_element_type=jnp.float32)
        if k == 0:
            gram[...] = part
        else:
            gram[...] += part
        out[k] = blocks[k, pl.ds(row, band), :]
    store_split(out, total, gram[pl.ds(row, width // USER), :])


def prepare(blocks, user):
    total, block, width = blocks.shape
    out = bf16(total + 2, block // USER, width)
    return pl.pallas_call(
        prepare_kernel,
        name="prepare",
        grid_spec=pltpu.PrefetchScalarGridSpec(
            num_scalar_prefetch=1,
            in_specs=[IN_VMEM],
            out_specs=IN_VMEM,
            scratch_shapes=[pltpu.VMEM((width, width), jnp.float32)],
        ),
        compiler_params=limit(8),
        out_shape=out,
    )(user.reshape(1), blocks)


def pick_kernel(offsets, wanted, place, *refs):
    pieces, out = refs[:-1], refs[-1]
    z = place[0]
    band = pieces[0].shape[1]
    for p in range(out.shape[0]):
        for slot, (source, offset) in enumerate(zip(pieces, offsets)):
            out[p, slot * band : (slot + 1) * band, :] = source[wanted[p, (z + offset) & (Z_SIZE - 1)]]


def pick(offsets, wanted, z, pieces):
    _, band, width = pieces[0].shape
    out = bf16(wanted.shape[0], len(offsets) * band, width)
    return pl.pallas_call(
        functools.partial(pick_kernel, offsets),
        name="pick",
        grid_spec=pltpu.PrefetchScalarGridSpec(
            num_scalar_prefetch=2,
            in_specs=[IN_VMEM] * len(pieces),
            out_specs=IN_VMEM,
        ),
        compiler_params=limit(4),
        out_shape=out,
    )(wanted, z.reshape(1), *pieces)


def gather_heads_kernel(head_ids, place, *refs):
    pieces, out = refs[:-1], refs[-1]
    total, band, width = pieces[0].shape
    per_shard = total - 2
    heads = head_ids.shape[0]
    for h in range(heads):
        block = head_ids[h]
        shift = (block // per_shard - place[0]) & (Z_SIZE - 1)
        for source, offset in zip(pieces, OFFSETS):

            @pl.when(shift == offset % Z_SIZE)
            def _():
                out[h] = source[block & (per_shard - 1)]

    gram = jnp.zeros((band, width), jnp.float32)
    for source in pieces:
        gram += source[per_shard].astype(jnp.float32) + source[per_shard + 1].astype(jnp.float32)
    store_split(out, heads, gram)


def gather_heads(head_ids, z, pieces):
    out = bf16(head_ids.shape[0] + 2, *pieces[0].shape[1:])
    return pl.pallas_call(
        gather_heads_kernel,
        name="gather_heads",
        grid_spec=pltpu.PrefetchScalarGridSpec(
            num_scalar_prefetch=2,
            in_specs=[IN_VMEM] * len(pieces),
            out_specs=IN_VMEM,
        ),
        compiler_params=limit(4),
        out_shape=out,
    )(head_ids, z.reshape(1), *pieces)


def merge_kernel(slabs, place, own, above, across, below, out):
    heads = slabs.shape[0]
    pieces = (own, above, across, below)
    for h in range(heads):
        shift = (slabs[h] - place[0]) & (Y_SIZE - 1)
        for other, source in enumerate(pieces):

            @pl.when(shift == other)
            def _():
                out[h] = source[h]

    gram = jnp.zeros(out.shape[1:], jnp.float32)
    for source in pieces:
        gram += source[heads].astype(jnp.float32) + source[heads + 1].astype(jnp.float32)
    store_split(out, heads, gram)


def merge(slabs, y, pieces):
    return pl.pallas_call(
        merge_kernel,
        name="merge",
        grid_spec=pltpu.PrefetchScalarGridSpec(
            num_scalar_prefetch=2,
            in_specs=[IN_VMEM] * len(pieces),
            out_specs=IN_VMEM,
        ),
        compiler_params=limit(4),
        out_shape=bf16(*pieces[0].shape),
    )(slabs, y.reshape(1), *pieces)


def weigh_kernel(head_counts, tail_counts, weights, counts, sems):
    heads, tails = head_counts.shape[1], tail_counts.shape[1]
    block = weights.shape[0]
    copies = [pltpu.make_async_copy(head_counts.at[0, k], counts.at[k], sems.at[k]) for k in range(heads)]
    copies += [pltpu.make_async_copy(tail_counts.at[0, k], counts.at[heads + k], sems.at[heads + k]) for k in range(tails)]
    for copy in copies:
        copy.start()

    def one_tile(k, carry):
        pltpu.make_async_copy(head_counts.at[0, 0], counts.at[k], sems.at[k]).wait()
        weight = conf_alpha * counts[k].astype(jnp.float32)
        weights[:, pl.ds(pl.multiple_of(k * block, block), block)] = weight.astype(jnp.bfloat16)
        return carry

    lax.fori_loop(0, heads + tails, one_tile, 0)


def weigh(head_counts, tail_counts):
    total, block = head_counts.shape[1] + tail_counts.shape[1], head_counts.shape[-1]
    return pl.pallas_call(
        weigh_kernel,
        name="weigh",
        in_specs=[pl.BlockSpec(memory_space=pltpu.HBM)] * 2,
        out_specs=IN_VMEM,
        out_shape=bf16(block, total * block),
        scratch_shapes=[pltpu.VMEM((total, block, block), jnp.int32), pltpu.SemaphoreType.DMA((total,))],
        compiler_params=limit(63),
    )(head_counts, tail_counts)


def solve_kernel(slab, slot, place, start, *refs):
    served, refs = refs[: len(PARTS)], refs[len(PARTS) :]
    same, other, weights_in, new_out, res_out, *refs = refs
    weights, tiles, scaled, gram, acc, tile_sems, gram_sems, head_sems, weight_sems = refs
    block, width = start.shape
    total = weights.shape[1] // block
    heads = same.shape[1] - 2
    tails = total - heads
    band = same.shape[2]

    gram_copies, head_copies = [], []
    x, core = place[0] // 2, place[0] % 2
    for i, source in enumerate((same, other)):
        for j in range(USER // 2):
            n = i * (USER // 2) + j
            user = ((x + j) & (USER // 2 - 1)) * 2 + (core if i == 0 else 1 - core)
            gram_copies.append(pltpu.make_async_copy(source.at[j, heads:], gram.at[:, user], gram_sems.at[n]))
            head_copies.append(pltpu.make_async_copy(source.at[j, :heads], tiles.at[:heads, user], head_sems.at[n]))

    chunk = weights.shape[1] // weight_sems.shape[0]
    weight_copies = [
        pltpu.make_async_copy(weights_in.at[:, pl.ds(n * chunk, chunk)], weights.at[:, pl.ds(n * chunk, chunk)], weight_sems.at[n])
        for n in range(weight_sems.shape[0])
    ]

    def tail_copy(k, part, any_rows=False):
        row = 0 if any_rows else pl.multiple_of((slot[k] - FIRST[part]) * band, band)
        return pltpu.make_async_copy(
            served[part].at[:, 0 if any_rows else slab[k], pl.ds(row, band), :], tiles.at[heads + k], tile_sems.at[heads + k]
        )

    for copy in gram_copies:
        copy.start()
    for copy in head_copies + weight_copies:
        copy.start()
    for k in range(tails):
        for part, offsets in enumerate(PARTS):

            @pl.when((slot[k] >= FIRST[part]) & (slot[k] < FIRST[part] + len(offsets)))
            def _():
                tail_copy(k, part).start()

    def tile_of(k):
        return tiles[k].reshape(block, width)

    def columns(k, count=1):
        return pl.ds(pl.multiple_of(k * block, block), count * block)

    def scores_of(rounded, tile):
        return lax.dot_general(rounded, tile, (((1,), (1,)), ((), ())), preferred_element_type=jnp.float32)

    def matmul(left, right):
        return jnp.dot(left, right, preferred_element_type=jnp.float32)

    def dense_part(vector, high):
        low = (vector - high.astype(jnp.float32)).astype(jnp.bfloat16)
        gram_high, gram_low = gram[0].reshape(width, width), gram[1].reshape(width, width)
        return matmul(high, gram_high) + (matmul(high, gram_low) + matmul(low, gram_high)) + ridge_term * vector

    def data_part(left, group):
        def some(i, carry):
            k = i * group
            rows = tiles[pl.ds(k, group)].reshape(group * block, width)
            acc[...] += matmul(left(columns(k, group)), rows)
            return carry

        lax.fori_loop(0, total // group, some, 0)

    def scores_part(rounded, first, count, wait=False):
        def some(i, carry):
            if wait:
                for j in range(4):
                    tail_copy(i * 4 + j, 0, True).wait()
            for j in range(4):
                k = first + i * 4 + j
                weight = weights[:, columns(k)].astype(jnp.float32)
                scaled[:, columns(k)] = (scores_of(rounded, tile_of(k)) * weight).astype(jnp.bfloat16)
            return carry

        lax.fori_loop(0, count // 4, some, 0)

    def apply_operator(vector):
        rounded = vector.astype(jnp.bfloat16)
        acc[...] = dense_part(vector, rounded)
        scores_part(rounded, 0, total)
        data_part(lambda at: scaled[:, at], 6)
        return acc[...]

    solution = start[...]
    rounded = solution.astype(jnp.bfloat16)

    def rated(at):
        weight = weights[:, at]
        return jnp.where(weight > 0, weight + 1, jnp.zeros_like(weight))

    for copy in gram_copies + head_copies + weight_copies:
        copy.wait()
    acc[...] = dense_part(solution, rounded)
    scores_part(rounded, 0, heads)
    scores_part(rounded, heads, tails, True)
    data_part(lambda at: scaled[:, at], 6)
    acc[...] = -acc[...]
    data_part(rated, 6)
    residual = acc[...]
    direction = residual
    norm_now = jnp.sum(residual * residual, axis=1, keepdims=True)
    for turn_index in range(ITERS):
        image = apply_operator(direction)
        step_size = norm_now / (jnp.sum(direction * image, axis=1, keepdims=True) + epsilon)
        solution = solution + step_size * direction
        residual = residual - step_size * image
        if turn_index + 1 < ITERS:
            norm_next = jnp.sum(residual * residual, axis=1, keepdims=True)
            direction = residual + norm_next / (norm_now + epsilon) * direction
            norm_now = norm_next
    new_out[...] = solution
    res_out[...] = residual


def solve(slab, slot, user, start, served, same, other, weights):
    block, width = start.shape
    band = same.shape[2]
    total = weights.shape[1] // block
    out = jax.ShapeDtypeStruct((block, width), jnp.float32)
    return pl.pallas_call(
        solve_kernel,
        name="solve",
        grid_spec=pltpu.PrefetchScalarGridSpec(
            num_scalar_prefetch=3,
            in_specs=[IN_VMEM] + [pl.BlockSpec(memory_space=pltpu.HBM)] * (len(served) + 3),
            out_specs=(IN_VMEM, IN_VMEM),
            scratch_shapes=[
                pltpu.VMEM((block, total * block), jnp.bfloat16),
                pltpu.VMEM((total, USER, band, width), jnp.bfloat16),
                pltpu.VMEM((block, total * block), jnp.bfloat16),
                pltpu.VMEM((2, USER, width // USER, width), jnp.bfloat16),
                pltpu.VMEM((block, width), jnp.float32),
                pltpu.SemaphoreType.DMA((total,)),
                pltpu.SemaphoreType.DMA((USER,)),
                pltpu.SemaphoreType.DMA((USER,)),
                pltpu.SemaphoreType.DMA((4,)),
            ],
        ),
        out_shape=(out, out),
        compiler_params=limit(63),
    )(slab, slot, user.reshape(1), start, *served, same, other, weights)


def ring(step, size=Z_SIZE):
    return [(i, (i + step) % size) for i in range(size)]


def line(step):
    return [(i, (i + 2 * step) % USER) for i in range(USER)]


def local(user_factors, item_factors, head_ids, tail_ids, head_counts, tail_counts):
    user, y, z = (lax.axis_index(axis) for axis in ALL)
    block_size = head_counts.shape[-1]
    width = item_factors.shape[1]
    per_shard = item_factors.shape[0] // block_size

    own = prepare(item_factors.reshape(per_shard, block_size, width), user)

    ids = tail_ids.reshape(-1)
    owner_of, local_of = ids // per_shard, ids % per_shard
    owners = jnp.arange(Y_SIZE * Z_SIZE, dtype=jnp.int32)
    requests = jnp.sum(jnp.where(owner_of[:, None] == owners[None, :], local_of[:, None], 0), axis=0)
    requests = jnp.tile(requests.reshape(Y_SIZE, Z_SIZE), (USER, 1))
    wanted = lax.all_to_all(requests, PLANE, 0, 0, tiled=True)

    up = down = own
    pieces = [own]
    for _ in range(1, 4):
        up = lax.ppermute(up, "z", ring(1))
        down = lax.ppermute(down, "z", ring(-1))
        pieces += [up, down]
    pieces.append(lax.ppermute(up, "z", ring(1)))

    served = []
    for part, offsets in enumerate(PARTS):
        picked = pick(offsets, wanted, z, pieces[FIRST[part] : FIRST[part] + len(offsets)])
        arrived = lax.all_to_all(picked, PLANE, 0, 0, tiled=True)
        served.append(arrived.reshape(USER, Y_SIZE, *arrived.shape[1:]))

    shared = gather_heads(head_ids, z, pieces)
    slabs = [shared] + [lax.ppermute(shared, "y", ring(-step, Y_SIZE)) for step in range(1, Y_SIZE)]
    merged = merge(head_ids // (per_shard * Z_SIZE), y, slabs)
    same = jnp.stack([merged] + [lax.ppermute(merged, "user", line(-step)) for step in range(1, USER // 2)])
    other = lax.ppermute(same, "user", [(i, i ^ 1) for i in range(USER)])

    weights = weigh(head_counts, tail_counts)
    slot = jnp.asarray(SLOT_OF_SHIFT, jnp.int32)[(owner_of - z) % Z_SIZE]
    return solve(owner_of // Z_SIZE, slot, user, user_factors, served, same, other, weights)


def solution(mesh):
    fine = Mesh(mesh.devices.reshape(USER, Y_SIZE, Z_SIZE), ALL)
    return jax.shard_map(
        local,
        mesh=fine,
        in_specs=(P(ALL, None), P(("y", "z"), None), P(), P(ALL, None), P(ALL, None, None, None), P(ALL, None, None, None)),
        out_specs=(P(ALL, None), P(ALL, None)),
        check_vma=False,
    )
```

time: 158 us -> 160 us (1.013)
  starting transfers between devices: 42 us -> 49.5 us
  local copies, waits for them, and re-layouts: 6.7 us -> 3.5 us
  Pallas kernels: 35.3 us -> 32.7 us
  waiting for transfers between devices: 69.3 us -> 71 us
    all_to_all x2 -> x3, waiting for transfers between devices: 0.01 us -> 13.6 us  [local(): arrived = lax.all_to_all(picked, PLANE, 0, 0, tiled=True)]
    ppermute x3, waiting for transfers between devices: 33.8 us -> 21.4 us  [local(): lax.ppermute(shared, 'y', ring(-step, Y_SIZE))]
    ppermute x3, waiting for transfers between devices: 0.01 us -> 6.27 us  [local(): down = lax.ppermute(down, 'z', ring(-1))]
    ppermute x3, waiting for transfers between devices: 13.2 us -> 7.23 us  [local(): up = lax.ppermute(up, 'z', ring(1))]
    all_to_all x2 -> x3, starting transfers between devices: 12.6 us -> 18.5 us  [local(): arrived = lax.all_to_all(picked, PLANE, 0, 0, tiled=True)]
    pallas_call x2 -> x5, Pallas kernels: 8.18 us -> 11.7 us  [the longest x3 6.13 us: pick(): pl.pallas_call(functools.partial(pick_kernel, offsets), name='pick', grid...]
    unnamed x40 -> x12, local copies, waits for them, and re-layouts: 4.84 us -> 1.61 us
    ppermute x3, starting transfers between devices: 10.4 us -> 12.9 us  [local(): down = lax.ppermute(down, 'z', ring(-1))]
  transfers between devices with their start and end apart: 17 -> 18, of which waited for: 11 -> 10; matrix products, arithmetic and copies ran while one was open for 3% -> 2% of each run, Pallas kernels for 5% -> 7%
where the time goes in v2:
time: 160 us; the launch traced here: 158 us
  waiting for transfers between devices  71 us (44%)
  starting transfers between devices  49.5 us (31%)
  Pallas kernels  32.7 us (20%)
  local copies, waits for them, and re-layouts  3.5 us (2%)
    ppermute x3, waiting for transfers between devices, local(): lax.ppermute(shared, 'y', ring(-step, Y_SIZE))  21.4 us
    pallas_call x1, Pallas kernels, solve(): pl.pallas_call(solve_kernel, name='solve', grid_spec=pltpu.PrefetchScalar...  19.5 us
    all_to_all x3, starting transfers between devices, local(): arrived = lax.all_to_all(picked, PLANE, 0, 0, tiled=True)  18.5 us
    all_to_all x3, waiting for transfers between devices, local(): arrived = lax.all_to_all(picked, PLANE, 0, 0, tiled=True)  13.6 us
    ppermute x3, starting transfers between devices, local(): down = lax.ppermute(down, 'z', ring(-1))  12.9 us
    ppermute x1, waiting for transfers between devices, local(): pieces.append(lax.ppermute(up, 'z', ring(1)))  9.78 us
    all_to_all x1, starting transfers between devices, local(): wanted = lax.all_to_all(requests, PLANE, 0, 0, tiled=True)  7.62 us
    ppermute x3, waiting for transfers between devices, local(): up = lax.ppermute(up, 'z', ring(1))  7.23 us
  transfers between devices with their start and end apart: 18, of which 10 were waited for; matrix products, arithmetic and copies ran while one was open for 2% of the time, Pallas kernels for 7%

profile of v2, /device:TPU:2, one launch (start us, length us, event | category | flops | bytes accessed | tf_op | source)
XLA Modules:
  0.0 158.4 jit_solution(3156049045710465082)
XLA Ops:
  0.7 1.6 copy-done
  3.0 5.9 %collective-permute-start.1 = (bf16[18,32,256]{2,1,0:T(8,128)(2,1)S(1)}, bf16[18,32,256]{2,1,0:T(8,128)(2,1)S(1)}, u32[]{:S(2)}, u32[]{:S(2)}) collective-permute-start(bf16[18,32,256]{2,1,0:T(8,128)(2,1)S(1)} %prepare.1.refs_0_), channel_id=1, source_target_pairs={{0,7},{1,0},{2,1},{3,2},{4,3},{5,4},{6,5},{7,6},{8,15},{9,8},{10,9... | collective-permute-start | bytes 884744 | tf_op jit(solution)/shard_map/ppermute | solution.py:371
  8.9 6.3 %collective-permute-done.1.refs_2_ = bf16[18,32,256]{2,1,0:T(8,128)(2,1)S(1)} collective-permute-done((bf16[18,32,256]{2,1,0:T(8,128)(2,1)S(1)}, bf16[18,32,256]{2,1,0:T(8,128)(2,1)S(1)}, u32[]{:S(2)}, u32[]{:S(2)}) %collective-permute-start.1) | collective-permute-done | bytes 294944 | tf_op jit(solution)/shard_map/ppermute | solution.py:371
  15.2 3.7 %collective-permute-start.3 = (bf16[18,32,256]{2,1,0:T(8,128)(2,1)S(1)}, bf16[18,32,256]{2,1,0:T(8,128)(2,1)S(1)}, u32[]{:S(2)}, u32[]{:S(2)}) collective-permute-start(bf16[18,32,256]{2,1,0:T(8,128)(2,1)S(1)} %collective-permute-done.1.refs_2_), channel_id=1, source_target_pairs={{0,7},{1,0},{2,1},{3,2},{4,3},{5,4},{6,5},{7,6},{8,15},{9,8},{10,9... | collective-permute-start | bytes 884744 | tf_op jit(solution)/shard_map/ppermute | solution.py:371
  20.2 7.6 %all-to-all-start = ((s32[32,1,8]{2,1,0:T(1,128)}), s32[32,1,8]{2,1,0:T(1,128)S(1)}, u32[]{:S(2)}, u32[]{:S(2)}) async-start(s32[32,1,8]{2,1,0:T(1,128)} %bitcast.4), calls=%async_computation | async-start | bytes 32768 | tf_op jit(solution)/shard_map/all_to_all | solution.py:365
  27.9 6.1 %all-to-all-done = s32[32,1,8]{2,1,0:T(1,128)S(1)} async-done(((s32[32,1,8]{2,1,0:T(1,128)}), s32[32,1,8]{2,1,0:T(1,128)S(1)}, u32[]{:S(2)}, u32[]{:S(2)}) %all-to-all-start) | async-done | bytes 1056 | tf_op jit(solution)/shard_map/all_to_all | solution.py:365
  34.0 1.9 %pick.4 = bf16[32,64,256]{2,1,0:T(8,128)(2,1)} custom-call(s32[32,8]{1,0:T(8,128)S(1)} %bitcast.43, s32[1]{0:T(128)} %bitcast.6.place, bf16[18,32,256]{2,1,0:T(8,128)(2,1)S(1)} %collective-permute-done.2.refs_0_.refs_3_, bf16[18,32,256]{2,1,0:T(8,128)(2,1)S(1)} %collective-permute-done.3.refs_1_.refs_4_), custom_call_target="tpu_custom_call" | custom-call | tf_op jit(solution)/shard_map/pick/pallas_call | solution.py:87
  35.9 5.0 %all-to-all-start.2 = ((bf16[32,64,256]{2,1,0:T(8,128)(2,1)}), bf16[32,64,256]{2,1,0:T(8,128)(2,1)S(1)}, u32[]{:S(2)}, u32[]{:S(2)}) async-start(bf16[32,64,256]{2,1,0:T(8,128)(2,1)} %pick.4), calls=%async_computation.2 | async-start | bytes 2097152 | tf_op jit(solution)/shard_map/all_to_all | solution.py:378
  40.9 2.1 %pick.3 = bf16[32,96,256]{2,1,0:T(8,128)(2,1)} custom-call(s32[32,8]{1,0:T(8,128)S(1)} %bitcast.44, s32[1]{0:T(128)} %bitcast.6.place, bf16[18,32,256]{2,1,0:T(8,128)(2,1)S(1)} %prepare.1.refs_0_, bf16[18,32,256]{2,1,0:T(8,128)(2,1)S(1)} %collective-permute-done.refs_1_, bf16[18,32,256]{2,1,0:T(8,128)(2,1)S(1)} %collective-permute-done.1.refs_2_), custom_call_target="tpu_custom_call" | custom-call | tf_op jit(solution)/shard_map/pick/pallas_call | solution.py:87
  43.1 13.6 %all-to-all-done.2 = bf16[32,64,256]{2,1,0:T(8,128)(2,1)S(1)} async-done(((bf16[32,64,256]{2,1,0:T(8,128)(2,1)}), bf16[32,64,256]{2,1,0:T(8,128)(2,1)S(1)}, u32[]{:S(2)}, u32[]{:S(2)}) %all-to-all-start.2) | async-done | bytes 1048608 | tf_op jit(solution)/shard_map/all_to_all | solution.py:378
  56.7 5.9 %all-to-all-start.1 = ((bf16[32,96,256]{2,1,0:T(8,128)(2,1)}), bf16[32,96,256]{2,1,0:T(8,128)(2,1)}, u32[]{:S(2)}, u32[]{:S(2)}) async-start(bf16[32,96,256]{2,1,0:T(8,128)(2,1)} %pick.3), calls=%async_computation.1 | async-start | bytes 3145728 | tf_op jit(solution)/shard_map/all_to_all | solution.py:378
  62.7 3.3 %collective-permute-start.5 = (bf16[18,32,256]{2,1,0:T(8,128)(2,1)S(1)}, bf16[18,32,256]{2,1,0:T(8,128)(2,1)S(1)}, u32[]{:S(2)}, u32[]{:S(2)}) collective-permute-start(bf16[18,32,256]{2,1,0:T(8,128)(2,1)S(1)} %collective-permute-done.3.refs_1_.refs_4_), channel_id=1, source_target_pairs={{0,7},{1,0},{2,1},{3,2},{4,3},{5,4},{6,5},{7,6},{8,15},{9,8},{10,9... | collective-permute-start | bytes 884744 | tf_op jit(solution)/shard_map/ppermute | solution.py:371
  66.0 7.2 %collective-permute-done.4.refs_0_.refs_5_ = bf16[18,32,256]{2,1,0:T(8,128)(2,1)S(1)} collective-permute-done((bf16[18,32,256]{2,1,0:T(8,128)(2,1)S(1)}, bf16[18,32,256]{2,1,0:T(8,128)(2,1)S(1)}, u32[]{:S(2)}, u32[]{:S(2)}) %collective-permute-start.4) | collective-permute-done | bytes 294944 | tf_op jit(solution)/shard_map/ppermute | solution.py:370
  73.2 9.8 %collective-permute-done.6.refs_2_.refs_7_ = bf16[18,32,256]{2,1,0:T(8,128)(2,1)S(1)} collective-permute-done((bf16[18,32,256]{2,1,0:T(8,128)(2,1)S(1)}, bf16[18,32,256]{2,1,0:T(8,128)(2,1)S(1)}, u32[]{:S(2)}, u32[]{:S(2)}) %collective-permute-start.6) | collective-permute-done | bytes 294944 | tf_op jit(solution)/shard_map/ppermute | solution.py:373
  83.0 2.1 %pick.5 = bf16[32,96,256]{2,1,0:T(8,128)(2,1)} custom-call(s32[32,8]{1,0:T(8,128)S(1)} %bitcast.45, s32[1]{0:T(128)} %bitcast.6.place, bf16[18,32,256]{2,1,0:T(8,128)(2,1)S(1)} %collective-permute-done.4.refs_0_.refs_5_, bf16[18,32,256]{2,1,0:T(8,128)(2,1)S(1)} %collective-permute-done.5.refs_1_.refs_6_, ...), custom_call_target="tpu_custom_call" | custom-call | tf_op jit(solution)/shard_map/pick/pallas_call | solution.py:87
  85.1 7.5 %all-to-all-start.3 = ((bf16[32,96,256]{2,1,0:T(8,128)(2,1)}), bf16[32,96,256]{2,1,0:T(8,128)(2,1)}, u32[]{:S(2)}, u32[]{:S(2)}) async-start(bf16[32,96,256]{2,1,0:T(8,128)(2,1)} %pick.5), calls=%async_computation.3 | async-start | bytes 3145728 | tf_op jit(solution)/shard_map/all_to_all | solution.py:378
  95.2 2.7 %collective-permute-start.8 = (bf16[10,32,256]{2,1,0:T(8,128)(2,1)S(1)}, bf16[10,32,256]{2,1,0:T(8,128)(2,1)S(1)}, u32[]{:S(2)}, u32[]{:S(2)}) collective-permute-start(bf16[10,32,256]{2,1,0:T(8,128)(2,1)S(1)} %gather_heads.1.own), channel_id=1, source_target_pairs={{0,16},{8,24},{16,0},{24,8},{1,17},{9,25},{17,1},{25,9},{2,18},{10... | collective-permute-start | bytes 491528 | tf_op jit(solution)/shard_map/ppermute | solution.py:382
  99.4 17.3 %collective-permute-done.9.below = bf16[10,32,256]{2,1,0:T(8,128)(2,1)S(1)} collective-permute-done((bf16[10,32,256]{2,1,0:T(8,128)(2,1)S(1)}, bf16[10,32,256]{2,1,0:T(8,128)(2,1)S(1)}, u32[]{:S(2)}, u32[]{:S(2)}) %collective-permute-start.9) | collective-permute-done | bytes 163872 | tf_op jit(solution)/shard_map/ppermute | solution.py:382
  116.7 4.1 %collective-permute-done.8.across = bf16[10,32,256]{2,1,0:T(8,128)(2,1)S(1)} collective-permute-done((bf16[10,32,256]{2,1,0:T(8,128)(2,1)S(1)}, bf16[10,32,256]{2,1,0:T(8,128)(2,1)S(1)}, u32[]{:S(2)}, u32[]{:S(2)}) %collective-permute-start.8) | collective-permute-done | bytes 163872 | tf_op jit(solution)/shard_map/ppermute | solution.py:382
  124.0 2.2 %collective-permute-start.10 = (bf16[10,32,256]{2,1,0:T(8,128)(2,1)S(1)}, bf16[10,32,256]{2,1,0:T(8,128)(2,1)S(1)}, u32[]{:S(2)}, u32[]{:S(2)}) collective-permute-start(bf16[10,32,256]{2,1,0:T(8,128)(2,1)S(1)} %merge.1), channel_id=1, source_target_pairs={{0,192},{32,224},{64,0},{96,32},{128,64},{160,96},{192,128},{224,1... | collective-permute-start | bytes 491528 | tf_op jit(solution)/shard_map/ppermute | solution.py:384
  126.1 2.4 %collective-permute-done.12 = bf16[10,32,256]{2,1,0:T(8,128)(2,1)S(1)} collective-permute-done((bf16[10,32,256]{2,1,0:T(8,128)(2,1)S(1)}, bf16[10,32,256]{2,1,0:T(8,128)(2,1)S(1)}, u32[]{:S(2)}, u32[]{:S(2)}) %collective-permute-start.12) | collective-permute-done | bytes 163872 | tf_op jit(solution)/shard_map/ppermute | solution.py:384
  128.5 2.9 %collective-permute-done.11 = bf16[10,32,256]{2,1,0:T(8,128)(2,1)S(1)} collective-permute-done((bf16[10,32,256]{2,1,0:T(8,128)(2,1)S(1)}, bf16[10,32,256]{2,1,0:T(8,128)(2,1)S(1)}, u32[]{:S(2)}, u32[]{:S(2)}) %collective-permute-start.11) | collective-permute-done | bytes 163872 | tf_op jit(solution)/shard_map/ppermute | solution.py:384
  134.1 4.6 %weigh.1.refs_5_ = bf16[256,6144]{1,0:T(8,128)(2,1)} custom-call(s32[1,8,256,256]{3,2,1,0:T(8,128)} %head_counts.1, s32[1,16,256,256]{3,2,1,0:T(8,128)} %tail_counts.1), custom_call_target="tpu_custom_call" | custom-call | tf_op jit(solution)/shard_map/weigh/pallas_call | solution.py:185
  138.8 19.5 %solve.1 = (f32[256,256]{1,0:T(8,128)}, f32[256,256]{1,0:T(8,128)}) custom-call(s32[16]{0:T(128)} %get-tuple-element.2.slab, s32[16]{0:T(128)} %gather_fusion, s32[1]{0:T(128)} %bitcast.3.place, f32[256,256]{1,0:T(8,128)} %start.1, bf16[8,4,96,256]{3,2,1,0:T(8,128)(2,1)} %bitcast.8.refs_0_, bf16[8,4,64,256]{3,2,1,0:T(8,128)(2,1)} %bitcast.46, ...), custom_call_target="tpu_custom_call" | custom-call | tf_op jit(solution)/shard_map/solve/pallas_call | solution.py:320
  (41 shorter events, 12.1 us)
Async XLA Ops:
  0.6 18.3 %copy-start.5 = (s32[1,16]{1,0:T(1,128)S(1)}, s32[1,16]{1,0:T(1,128)}, u32[]{:S(2)}) copy-start(s32[1,16]{1,0:T(1,128)} %param.10) | copy-start | bytes 196
  0.6 1.6 %copy-start = (bf16[4096,256]{1,0:T(8,128)(2,1)S(1)}, bf16[4096,256]{1,0:T(8,128)(2,1)}, u32[]{:S(2)}) copy-start(bf16[4096,256]{1,0:T(8,128)(2,1)} %param.8) | copy-start | bytes 6291460
  3.0 12.2 %collective-permute-start.1 = (bf16[18,32,256]{2,1,0:T(8,128)(2,1)S(1)}, bf16[18,32,256]{2,1,0:T(8,128)(2,1)S(1)}, u32[]{:S(2)}, u32[]{:S(2)}) collective-permute-start(bf16[18,32,256]{2,1,0:T(8,128)(2,1)S(1)} %prepare.1.refs_0_), channel_id=1, source_target_pairs={{0,7},{1,0},{2,1},{3,2},{4,3},{5,4},{6,5},{7,6},{8,15},{9,8},{10,9... | collective-permute-start | bytes 884744 | tf_op jit(solution)/shard_map/ppermute | solution.py:371
  8.9 10.0 %collective-permute-start = (bf16[18,32,256]{2,1,0:T(8,128)(2,1)S(1)}, bf16[18,32,256]{2,1,0:T(8,128)(2,1)S(1)}, u32[]{:S(2)}, u32[]{:S(2)}) collective-permute-start(bf16[18,32,256]{2,1,0:T(8,128)(2,1)S(1)} %prepare.1.refs_0_), channel_id=1, source_target_pairs={{0,1},{1,2},{2,3},{3,4},{4,5},{5,6},{6,7},{7,0},{8,9},{9,10},{10,1... | collective-permute-start | bytes 884744 | tf_op jit(solution)/shard_map/ppermute | solution.py:370
  15.2 18.8 %collective-permute-start.3 = (bf16[18,32,256]{2,1,0:T(8,128)(2,1)S(1)}, bf16[18,32,256]{2,1,0:T(8,128)(2,1)S(1)}, u32[]{:S(2)}, u32[]{:S(2)}) collective-permute-start(bf16[18,32,256]{2,1,0:T(8,128)(2,1)S(1)} %collective-permute-done.1.refs_2_), channel_id=1, source_target_pairs={{0,7},{1,0},{2,1},{3,2},{4,3},{5,4},{6,5},{7,6},{8,15},{9,8},{10,9... | collective-permute-start | bytes 884744 | tf_op jit(solution)/shard_map/ppermute | solution.py:371
  18.9 15.1 %collective-permute-start.2 = (bf16[18,32,256]{2,1,0:T(8,128)(2,1)S(1)}, bf16[18,32,256]{2,1,0:T(8,128)(2,1)S(1)}, u32[]{:S(2)}, u32[]{:S(2)}) collective-permute-start(bf16[18,32,256]{2,1,0:T(8,128)(2,1)S(1)} %collective-permute-done.refs_1_), channel_id=1, source_target_pairs={{0,1},{1,2},{2,3},{3,4},{4,5},{5,6},{6,7},{7,0},{8,9},{9,10},{10,1... | collective-permute-start | bytes 884744 | tf_op jit(solution)/shard_map/ppermute | solution.py:370
  20.2 13.7 %all-to-all-start = ((s32[32,1,8]{2,1,0:T(1,128)}), s32[32,1,8]{2,1,0:T(1,128)S(1)}, u32[]{:S(2)}, u32[]{:S(2)}) async-start(s32[32,1,8]{2,1,0:T(1,128)} %bitcast.4), calls=%async_computation | async-start | bytes 32768 | tf_op jit(solution)/shard_map/all_to_all | solution.py:365
  35.9 20.8 %all-to-all-start.2 = ((bf16[32,64,256]{2,1,0:T(8,128)(2,1)}), bf16[32,64,256]{2,1,0:T(8,128)(2,1)S(1)}, u32[]{:S(2)}, u32[]{:S(2)}) async-start(bf16[32,64,256]{2,1,0:T(8,128)(2,1)} %pick.4), calls=%async_computation.2 | async-start | bytes 2097152 | tf_op jit(solution)/shard_map/all_to_all | solution.py:378
  56.7 28.5 %copy-start.3 = (bf16[32,64,256]{2,1,0:T(8,128)(2,1)}, bf16[32,64,256]{2,1,0:T(8,128)(2,1)S(1)}, u32[]{:S(2)}) copy-start(bf16[32,64,256]{2,1,0:T(8,128)(2,1)S(1)} %all-to-all-done.2) | copy-start | bytes 3145732
  56.7 28.5 %all-to-all-start.1 = ((bf16[32,96,256]{2,1,0:T(8,128)(2,1)}), bf16[32,96,256]{2,1,0:T(8,128)(2,1)}, u32[]{:S(2)}, u32[]{:S(2)}) async-start(bf16[32,96,256]{2,1,0:T(8,128)(2,1)} %pick.3), calls=%async_computation.1 | async-start | bytes 3145728 | tf_op jit(solution)/shard_map/all_to_all | solution.py:378
  62.6 10.6 %collective-permute-start.4 = (bf16[18,32,256]{2,1,0:T(8,128)(2,1)S(1)}, bf16[18,32,256]{2,1,0:T(8,128)(2,1)S(1)}, u32[]{:S(2)}, u32[]{:S(2)}) collective-permute-start(bf16[18,32,256]{2,1,0:T(8,128)(2,1)S(1)} %collective-permute-done.2.refs_0_.refs_3_), channel_id=1, source_target_pairs={{0,1},{1,2},{2,3},{3,4},{4,5},{5,6},{6,7},{7,0},{8,9},{9,10},{10,1... | collective-permute-start | bytes 884744 | tf_op jit(solution)/shard_map/ppermute | solution.py:370
  62.7 10.5 %collective-permute-start.5 = (bf16[18,32,256]{2,1,0:T(8,128)(2,1)S(1)}, bf16[18,32,256]{2,1,0:T(8,128)(2,1)S(1)}, u32[]{:S(2)}, u32[]{:S(2)}) collective-permute-start(bf16[18,32,256]{2,1,0:T(8,128)(2,1)S(1)} %collective-permute-done.3.refs_1_.refs_4_), channel_id=1, source_target_pairs={{0,7},{1,0},{2,1},{3,2},{4,3},{5,4},{6,5},{7,6},{8,15},{9,8},{10,9... | collective-permute-start | bytes 884744 | tf_op jit(solution)/shard_map/ppermute | solution.py:371
  73.2 9.8 %collective-permute-start.6 = (bf16[18,32,256]{2,1,0:T(8,128)(2,1)S(1)}, bf16[18,32,256]{2,1,0:T(8,128)(2,1)S(1)}, u32[]{:S(2)}, u32[]{:S(2)}) collective-permute-start(bf16[18,32,256]{2,1,0:T(8,128)(2,1)S(1)} %collective-permute-done.4.refs_0_.refs_5_), channel_id=1, source_target_pairs={{0,1},{1,2},{2,3},{3,4},{4,5},{5,6},{6,7},{7,0},{8,9},{9,10},{10,1... | collective-permute-start | bytes 884744 | tf_op jit(solution)/shard_map/ppermute | solution.py:373
  85.1 7.5 %copy-start.1 = (s32[8]{0:T(128)S(1)}, s32[8]{0:T(128)}, u32[]{:S(2)}) copy-start(s32[8]{0:T(128)} %head_ids.1) | copy-start | bytes 100
  85.1 53.7 %all-to-all-start.3 = ((bf16[32,96,256]{2,1,0:T(8,128)(2,1)}), bf16[32,96,256]{2,1,0:T(8,128)(2,1)}, u32[]{:S(2)}, u32[]{:S(2)}) async-start(bf16[32,96,256]{2,1,0:T(8,128)(2,1)} %pick.5), calls=%async_computation.3 | async-start | bytes 3145728 | tf_op jit(solution)/shard_map/all_to_all | solution.py:378
  92.7 40.3 %copy-start.2 = (s32[8]{0:T(128)S(1)}, s32[8]{0:T(128)}, u32[]{:S(2)}) copy-start(s32[8]{0:T(128)} %constant.77.clone) | copy-start | bytes 100
  93.7 23.0 %collective-permute-start.9 = (bf16[10,32,256]{2,1,0:T(8,128)(2,1)S(1)}, bf16[10,32,256]{2,1,0:T(8,128)(2,1)S(1)}, u32[]{:S(2)}, u32[]{:S(2)}) collective-permute-start(bf16[10,32,256]{2,1,0:T(8,128)(2,1)S(1)} %gather_heads.1.own), channel_id=1, source_target_pairs={{0,8},{8,16},{16,24},{24,0},{1,9},{9,17},{17,25},{25,1},{2,10},{10... | collective-permute-start | bytes 491528 | tf_op jit(solution)/shard_map/ppermute | solution.py:382
  95.2 25.5 %collective-permute-start.8 = (bf16[10,32,256]{2,1,0:T(8,128)(2,1)S(1)}, bf16[10,32,256]{2,1,0:T(8,128)(2,1)S(1)}, u32[]{:S(2)}, u32[]{:S(2)}) collective-permute-start(bf16[10,32,256]{2,1,0:T(8,128)(2,1)S(1)} %gather_heads.1.own), channel_id=1, source_target_pairs={{0,16},{8,24},{16,0},{24,8},{1,17},{9,25},{17,1},{25,9},{2,18},{10... | collective-permute-start | bytes 491528 | tf_op jit(solution)/shard_map/ppermute | solution.py:382
  97.9 22.9 %collective-permute-start.7 = (bf16[10,32,256]{2,1,0:T(8,128)(2,1)S(1)}, bf16[10,32,256]{2,1,0:T(8,128)(2,1)S(1)}, u32[]{:S(2)}, u32[]{:S(2)}) collective-permute-start(bf16[10,32,256]{2,1,0:T(8,128)(2,1)S(1)} %gather_heads.1.own), channel_id=1, source_target_pairs={{0,24},{8,0},{16,8},{24,16},{1,25},{9,1},{17,9},{25,17},{2,26},{10... | collective-permute-start | bytes 491528 | tf_op jit(solution)/shard_map/ppermute | solution.py:382
  121.5 7.0 %collective-permute-start.12 = (bf16[10,32,256]{2,1,0:T(8,128)(2,1)S(1)}, bf16[10,32,256]{2,1,0:T(8,128)(2,1)S(1)}, u32[]{:S(2)}, u32[]{:S(2)}) collective-permute-start(bf16[10,32,256]{2,1,0:T(8,128)(2,1)S(1)} %merge.1), channel_id=1, source_target_pairs={{0,64},{32,96},{64,128},{96,160},{128,192},{160,224},{192,0},{224,... | collective-permute-start | bytes 491528 | tf_op jit(solution)/shard_map/ppermute | solution.py:384
  122.8 8.6 %collective-permute-start.11 = (bf16[10,32,256]{2,1,0:T(8,128)(2,1)S(1)}, bf16[10,32,256]{2,1,0:T(8,128)(2,1)S(1)}, u32[]{:S(2)}, u32[]{:S(2)}) collective-permute-start(bf16[10,32,256]{2,1,0:T(8,128)(2,1)S(1)} %merge.1), channel_id=1, source_target_pairs={{0,128},{32,160},{64,192},{96,224},{128,0},{160,32},{192,64},{224,... | collective-permute-start | bytes 491528 | tf_op jit(solution)/shard_map/ppermute | solution.py:384
  124.0 8.7 %collective-permute-start.10 = (bf16[10,32,256]{2,1,0:T(8,128)(2,1)S(1)}, bf16[10,32,256]{2,1,0:T(8,128)(2,1)S(1)}, u32[]{:S(2)}, u32[]{:S(2)}) collective-permute-start(bf16[10,32,256]{2,1,0:T(8,128)(2,1)S(1)} %merge.1), channel_id=1, source_target_pairs={{0,192},{32,224},{64,0},{96,32},{128,64},{160,96},{192,128},{224,1... | collective-permute-start | bytes 491528 | tf_op jit(solution)/shard_map/ppermute | solution.py:384
  132.8 6.0 %copy-start.4 = (bf16[4,10,32,256]{3,2,1,0:T(8,128)(2,1)}, bf16[4,10,32,256]{3,2,1,0:T(8,128)(2,1)S(1)}, u32[]{:S(2)}) copy-start(bf16[4,10,32,256]{3,2,1,0:T(8,128)(2,1)S(1)} %pad_maximum_fusion.refs_3_) | copy-start | bytes 1966084
  132.8 6.0 %collective-permute-start.13 = (bf16[4,10,32,256]{3,2,1,0:T(8,128)(2,1)S(1)}, bf16[4,10,32,256]{3,2,1,0:T(8,128)(2,1)}, u32[]{:S(2)}, u32[]{:S(2)}) collective-permute-start(bf16[4,10,32,256]{3,2,1,0:T(8,128)(2,1)S(1)} %pad_maximum_fusion.refs_3_), channel_id=1, source_target_pairs={{0,32},{32,0},{64,96},{96,64},{128,160},{160,128},{192,224},{224,1... | collective-permute-start | bytes 1966088 | tf_op jit(solution)/shard_map/ppermute | solution.py:385

commit v3 on v2

--- a/solution.py
+++ b/solution.py
@@ -163,44 +163,50 @@
     )(slabs, y.reshape(1), *pieces)
 
 
-def weigh_kernel(head_counts, tail_counts, weights, counts, sems):
+def matmul(left, right):
+    return jnp.dot(left, right, preferred_element_type=jnp.float32)
+
+
+def scores_of(rounded, tile):
+    return lax.dot_general(rounded, tile, (((1,), (1,)), ((), ())), preferred_element_type=jnp.float32)
+
+
+def dense_part(vector, high, gram):
+    low = (vector - high.astype(jnp.float32)).astype(jnp.bfloat16)
+    width = vector.shape[1]
+    gram_high, gram_low = gram[0].reshape(width, width), gram[1].reshape(width, width)
+    return matmul(high, gram_high) + (matmul(high, gram_low) + matmul(low, gram_high)) + ridge_term * vector
+
+
+def columns(k, block, count=1):
+    return pl.ds(pl.multiple_of(k * block, block), count * block)
+
+
+def first_pass(acc, rounded, tiles, weights, first, pairs):
+    block = rounded.shape[0]
+
+    def some(i, carry):
+        part = None
+        for j in range(2):
+            k = first + i * 2 + j
+            tile = tiles[k].reshape(block, -1)
+            weight = weights[:, columns(k, block)]
+            rated = jnp.where(weight > 0, weight + 1, jnp.zeros_like(weight))
+            scaled = (scores_of(rounded, tile) * -weight.astype(jnp.float32)).astype(jnp.bfloat16)
+            data = matmul(rated, tile) + matmul(scaled, tile)
+            part = data if part is None else part + data
+        acc[...] += part
+        return carry
+
+    lax.fori_loop(0, pairs, some, 0)
+
+
+def warm_kernel(order, slab, slot, early, place, start, *refs):
+    served, refs = refs[: len(PARTS) - 1], refs[len(PARTS) - 1 :]
+    same, other, head_counts, tail_counts, weights, tiles, gram, partial, *refs = refs
+    counts, count_sems, tile_sems, gram_sems, head_sems = refs
     heads, tails = head_counts.shape[1], tail_counts.shape[1]
-    block = weights.shape[0]
-    copies = [pltpu.make_async_copy(head_counts.at[0, k], counts.at[k], sems.at[k]) for k in range(heads)]
-    copies += [pltpu.make_async_copy(tail_counts.at[0, k], counts.at[heads + k], sems.at[heads + k]) for k in range(tails)]
-    for copy in copies:
-        copy.start()
-
-    def one_tile(k, carry):
-        pltpu.make_async_copy(head_counts.at[0, 0], counts.at[k], sems.at[k]).wait()
-        weight = conf_alpha * counts[k].astype(jnp.float32)
-        weights[:, pl.ds(pl.multiple_of(k * block, block), block)] = weight.astype(jnp.bfloat16)
-        return carry
-
-    lax.fori_loop(0, heads + tails, one_tile, 0)
-
-
-def weigh(head_counts, tail_counts):
-    total, block = head_counts.shape[1] + tail_counts.shape[1], head_counts.shape[-1]
-    return pl.pallas_call(
-        weigh_kernel,
-        name="weigh",
-        in_specs=[pl.BlockSpec(memory_space=pltpu.HBM)] * 2,
-        out_specs=IN_VMEM,
-        out_shape=bf16(block, total * block),
-        scratch_shapes=[pltpu.VMEM((total, block, block), jnp.int32), pltpu.SemaphoreType.DMA((total,))],
-        compiler_params=limit(63),
-    )(head_counts, tail_counts)
-
-
-def solve_kernel(slab, slot, place, start, *refs):
-    served, refs = refs[: len(PARTS)], refs[len(PARTS) :]
-    same, other, weights_in, new_out, res_out, *refs = refs
-    weights, tiles, scaled, gram, acc, tile_sems, gram_sems, head_sems, weight_sems = refs
-    block, width = start.shape
-    total = weights.shape[1] // block
-    heads = same.shape[1] - 2
-    tails = total - heads
+    block = start.shape[0]
     band = same.shape[2]
 
     gram_copies, head_copies = [], []
@@ -211,91 +217,153 @@
             user = ((x + j) & (USER // 2 - 1)) * 2 + (core if i == 0 else 1 - core)
             gram_copies.append(pltpu.make_async_copy(source.at[j, heads:], gram.at[:, user], gram_sems.at[n]))
             head_copies.append(pltpu.make_async_copy(source.at[j, :heads], tiles.at[:heads, user], head_sems.at[n]))
-
-    chunk = weights.shape[1] // weight_sems.shape[0]
-    weight_copies = [
-        pltpu.make_async_copy(weights_in.at[:, pl.ds(n * chunk, chunk)], weights.at[:, pl.ds(n * chunk, chunk)], weight_sems.at[n])
-        for n in range(weight_sems.shape[0])
+    count_copies = [pltpu.make_async_copy(head_counts.at[0, k], counts.at[k], count_sems.at[k]) for k in range(heads)]
+    count_copies += [
+        pltpu.make_async_copy(tail_counts.at[0, order[k]], counts.at[heads + k], count_sems.at[heads + k])
+        for k in range(tails)
     ]
 
-    def tail_copy(k, part, any_rows=False):
-        row = 0 if any_rows else pl.multiple_of((slot[k] - FIRST[part]) * band, band)
+    def tail_copy(k, part):
+        row = pl.multiple_of((slot[k] - FIRST[part]) * band, band)
         return pltpu.make_async_copy(
-            served[part].at[:, 0 if any_rows else slab[k], pl.ds(row, band), :], tiles.at[heads + k], tile_sems.at[heads + k]
+            served[part].at[:, slab[k], pl.ds(row, band), :], tiles.at[heads + k], tile_sems.at[k]
         )
 
-    for copy in gram_copies:
-        copy.start()
-    for copy in head_copies + weight_copies:
+    for copy in gram_copies + head_copies + count_copies:
         copy.start()
     for k in range(tails):
-        for part, offsets in enumerate(PARTS):
-
-            @pl.when((slot[k] >= FIRST[part]) & (slot[k] < FIRST[part] + len(offsets)))
+        for part in range(len(PARTS) - 1):
+
+            @pl.when((slot[k] >= FIRST[part]) & (slot[k] < FIRST[part + 1]))
             def _():
                 tail_copy(k, part).start()
 
-    def tile_of(k):
-        return tiles[k].reshape(block, width)
-
-    def columns(k, count=1):
-        return pl.ds(pl.multiple_of(k * block, block), count * block)
-
-    def scores_of(rounded, tile):
-        return lax.dot_general(rounded, tile, (((1,), (1,)), ((), ())), preferred_element_type=jnp.float32)
-
-    def matmul(left, right):
-        return jnp.dot(left, right, preferred_element_type=jnp.float32)
-
-    def dense_part(vector, high):
-        low = (vector - high.astype(jnp.float32)).astype(jnp.bfloat16)
-        gram_high, gram_low = gram[0].reshape(width, width), gram[1].reshape(width, width)
-        return matmul(high, gram_high) + (matmul(high, gram_low) + matmul(low, gram_high)) + ridge_term * vector
-
-    def data_part(left, group):
-        def some(i, carry):
-            k = i * group
-            rows = tiles[pl.ds(k, group)].reshape(group * block, width)
-            acc[...] += matmul(left(columns(k, group)), rows)
-            return carry
-
-        lax.fori_loop(0, total // group, some, 0)
-
-    def scores_part(rounded, first, count, wait=False):
-        def some(i, carry):
-            if wait:
-                for j in range(4):
-                    tail_copy(i * 4 + j, 0, True).wait()
-            for j in range(4):
-                k = first + i * 4 + j
-                weight = weights[:, columns(k)].astype(jnp.float32)
-                scaled[:, columns(k)] = (scores_of(rounded, tile_of(k)) * weight).astype(jnp.bfloat16)
-            return carry
-
-        lax.fori_loop(0, count // 4, some, 0)
+    def one_tile(k, carry):
+        pltpu.make_async_copy(head_counts.at[0, 0], counts.at[k], count_sems.at[k]).wait()
+        weights[:, columns(k, block)] = (conf_alpha * counts[k].astype(jnp.float32)).astype(jnp.bfloat16)
+        return carry
+
+    lax.fori_loop(0, heads + tails, one_tile, 0)
+    for copy in gram_copies + head_copies:
+        copy.wait()
+    for k in range(tails):
+
+        @pl.when(slot[k] < FIRST[-1])
+        def _():
+            pltpu.make_async_copy(served[0].at[:, 0, pl.ds(0, band), :], tiles.at[heads + k], tile_sems.at[k]).wait()
+
+    vector = start[...]
+    rounded = vector.astype(jnp.bfloat16)
+    partial[...] = -dense_part(vector, rounded, gram)
+    first_pass(partial, rounded, tiles, weights, 0, (heads + early[0]) // 2)
+
+
+def warm(sorted_tails, user, start, served, same, other, head_counts, tail_counts):
+    block, width = start.shape
+    band = same.shape[2]
+    heads, tails = head_counts.shape[1], tail_counts.shape[1]
+    total = heads + tails
+    return pl.pallas_call(
+        warm_kernel,
+        name="warm",
+        grid_spec=pltpu.PrefetchScalarGridSpec(
+            num_scalar_prefetch=5,
+            in_specs=[IN_VMEM] + [pl.BlockSpec(memory_space=pl.ANY)] * (len(served) + 4),
+            out_specs=(IN_VMEM,) * 4,
+            scratch_shapes=[
+                pltpu.VMEM((total, block, block), jnp.int32),
+                pltpu.SemaphoreType.DMA((total,)),
+                pltpu.SemaphoreType.DMA((tails,)),
+                pltpu.SemaphoreType.DMA((USER,)),
+                pltpu.SemaphoreType.DMA((USER,)),
+            ],
+        ),
+        out_shape=(
+            bf16(block, total * block),
+            bf16(total, USER, band, width),
+            bf16(2, USER, width // USER, width),
+            jax.ShapeDtypeStruct((block, width), jnp.float32),
+        ),
+        compiler_params=limit(63),
+    )(*sorted_tails, user.reshape(1), start, *served, same, other, head_counts, tail_counts)
+
+
+def solve_kernel(slab, slot, early, start, weights_in, tiles_in, gram_in, partial, served, new_out, res_out, *refs):
+    weights, tiles, gram, acc, scaled, weight_sems, tile_sems, small_sems = refs
+    block, width = start.shape
+    total = tiles.shape[0]
+    tails = slab.shape[0]
+    heads = total - tails
+    band = tiles.shape[2]
+
+    small_copies = [pltpu.make_async_copy(partial, acc, small_sems.at[0]), pltpu.make_async_copy(gram_in, gram, small_sems.at[1])]
+    chunks = weight_sems.shape[0]
+    chunk = weights.shape[1] // chunks
+    weight_copies = [
+        pltpu.make_async_copy(weights_in.at[:, n * chunk : (n + 1) * chunk], weights.at[:, n * chunk : (n + 1) * chunk], weight_sems.at[n])
+        for n in range(chunks)
+    ]
+
+    def early_copy(k):
+        return pltpu.make_async_copy(tiles_in.at[k], tiles.at[k], tile_sems.at[k])
+
+    def late_copy(k):
+        row = pl.multiple_of((slot[k] - FIRST[-1]) * band, band)
+        return pltpu.make_async_copy(
+            served.at[:, slab[k], pl.ds(row, band), :], tiles.at[heads + k], tile_sems.at[heads + k]
+        )
+
+    small_copies[0].start()
+    for k in reversed(range(tails)):
+
+        @pl.when(slot[k] >= FIRST[-1])
+        def _():
+            late_copy(k).start()
+
+    for copy in reversed(weight_copies):
+        copy.start()
+    small_copies[1].start()
+    for k in range(heads):
+        early_copy(k).start()
+    for k in range(tails):
+
+        @pl.when(slot[k] < FIRST[-1])
+        def _():
+            early_copy(heads + k).start()
+
+    def tile_wait(k, carry):
+        pltpu.make_async_copy(tiles_in.at[0], tiles.at[k], tile_sems.at[k]).wait()
+        return carry
 
     def apply_operator(vector):
         rounded = vector.astype(jnp.bfloat16)
-        acc[...] = dense_part(vector, rounded)
-        scores_part(rounded, 0, total)
-        data_part(lambda at: scaled[:, at], 6)
+        acc[...] = dense_part(vector, rounded, gram)
+
+        def some_scores(i, carry):
+            for j in range(4):
+                k = i * 4 + j
+                weight = weights[:, columns(k, block)].astype(jnp.float32)
+                scores = scores_of(rounded, tiles[k].reshape(block, width))
+                scaled[:, columns(k, block)] = (scores * weight).astype(jnp.bfloat16)
+            return carry
+
+        def some_data(i, carry):
+            k = i * 6
+            acc[...] += matmul(scaled[:, columns(k, block, 6)], tiles[pl.ds(k, 6)].reshape(6 * block, width))
+            return carry
+
+        lax.fori_loop(0, total // 4, some_scores, 0)
+        lax.fori_loop(0, total // 6, some_data, 0)
         return acc[...]
 
     solution = start[...]
-    rounded = solution.astype(jnp.bfloat16)
-
-    def rated(at):
-        weight = weights[:, at]
-        return jnp.where(weight > 0, weight + 1, jnp.zeros_like(weight))
-
-    for copy in gram_copies + head_copies + weight_copies:
+    lax.fori_loop(heads + early[0], total, tile_wait, 0)
+    for copy in reversed(weight_copies):
         copy.wait()
-    acc[...] = dense_part(solution, rounded)
-    scores_part(rounded, 0, heads)
-    scores_part(rounded, heads, tails, True)
-    data_part(lambda at: scaled[:, at], 6)
-    acc[...] = -acc[...]
-    data_part(rated, 6)
+    small_copies[0].wait()
+    first_pass(acc, solution.astype(jnp.bfloat16), tiles, weights, heads + early[0], (tails - early[0]) // 2)
+    lax.fori_loop(0, heads + early[0], tile_wait, 0)
+    small_copies[1].wait()
     residual = acc[...]
     direction = residual
     norm_now = jnp.sum(residual * residual, axis=1, keepdims=True)
@@ -312,33 +380,28 @@
     res_out[...] = residual
 
 
-def solve(slab, slot, user, start, served, same, other, weights):
+def solve(slab, slot, early, start, warmed, served):
     block, width = start.shape
-    band = same.shape[2]
-    total = weights.shape[1] // block
+    weights, tiles = warmed[:2]
     out = jax.ShapeDtypeStruct((block, width), jnp.float32)
     return pl.pallas_call(
         solve_kernel,
         name="solve",
         grid_spec=pltpu.PrefetchScalarGridSpec(
             num_scalar_prefetch=3,
-            in_specs=[IN_VMEM] + [pl.BlockSpec(memory_space=pltpu.HBM)] * (len(served) + 3),
+            in_specs=[IN_VMEM] + [pl.BlockSpec(memory_space=pl.ANY)] * (1 + len(warmed)),
             out_specs=(IN_VMEM, IN_VMEM),
-            scratch_shapes=[
-                pltpu.VMEM((block, total * block), jnp.bfloat16),
-                pltpu.VMEM((total, USER, band, width), jnp.bfloat16),
-                pltpu.VMEM((block, total * block), jnp.bfloat16),
-                pltpu.VMEM((2, USER, width // USER, width), jnp.bfloat16),
-                pltpu.VMEM((block, width), jnp.float32),
-                pltpu.SemaphoreType.DMA((total,)),
-                pltpu.SemaphoreType.DMA((USER,)),
-                pltpu.SemaphoreType.DMA((USER,)),
+            scratch_shapes=[pltpu.VMEM(array.shape, array.dtype) for array in warmed]
+            + [
+                pltpu.VMEM(weights.shape, jnp.bfloat16),
                 pltpu.SemaphoreType.DMA((4,)),
+                pltpu.SemaphoreType.DMA((tiles.shape[0],)),
+                pltpu.SemaphoreType.DMA((2,)),
             ],
         ),
         out_shape=(out, out),
         compiler_params=limit(63),
-    )(slab, slot, user.reshape(1), start, *served, same, other, weights)
+    )(slab, slot, early, start, *warmed, served)
 
 
 def ring(step, size=Z_SIZE):
@@ -379,14 +442,29 @@
         served.append(arrived.reshape(USER, Y_SIZE, *arrived.shape[1:]))
 
     shared = gather_heads(head_ids, z, pieces)
-    slabs = [shared] + [lax.ppermute(shared, "y", ring(-step, Y_SIZE)) for step in range(1, Y_SIZE)]
+    slabs = [shared]
+    for step in range(1, Y_SIZE):
+        slabs.append(lax.ppermute(shared, "y", ring(-step, Y_SIZE)))
     merged = merge(head_ids // (per_shard * Z_SIZE), y, slabs)
-    same = jnp.stack([merged] + [lax.ppermute(merged, "user", line(-step)) for step in range(1, USER // 2)])
+    same = [merged]
+    for step in range(1, USER // 2):
+        same.append(lax.ppermute(merged, "user", line(-step)))
+    same = jnp.stack(same)
     other = lax.ppermute(same, "user", [(i, i ^ 1) for i in range(USER)])
 
-    weights = weigh(head_counts, tail_counts)
     slot = jnp.asarray(SLOT_OF_SHIFT, jnp.int32)[(owner_of - z) % Z_SIZE]
-    return solve(owner_of // Z_SIZE, slot, user, user_factors, served, same, other, weights)
+    late = slot >= FIRST[-1]
+    index = jnp.arange(slot.shape[0], dtype=jnp.int32)
+    before = (index[None, :] < index[:, None]) | (late[:, None] & ~late[None, :])
+    before &= ~(late[None, :] & ~late[:, None])
+    place = jnp.sum(before.astype(jnp.int32), axis=1)
+    table = place[:, None] == index[None, :]
+    order, slab, slot = (
+        jnp.sum(jnp.where(table, values[:, None], 0), axis=0) for values in (index, owner_of // Z_SIZE, slot)
+    )
+    early = (jnp.sum((~late).astype(jnp.int32)) & -2).reshape(1)
+    warmed = warm((order, slab, slot, early), user, user_factors, served[:-1], same, other, head_counts, tail_counts)
+    return solve(slab, slot, early, user_factors, warmed, served[-1])
 
 
 def solution(mesh):

time: 160 us -> 169 us (1.056)
  the two profiles are of different devices: /device:TPU:2 before, /device:TPU:1 now
where the time goes in v3:
time: 169 us
  waiting for transfers between devices  77.6 us (46%)
  starting transfers between devices  46 us (27%)
  Pallas kernels  37.9 us (22%)
  local copies, waits for them, and re-layouts  3.87 us (2%)
  other arithmetic  1.73 us (1%)
    ppermute x3, waiting for transfers between devices, local(): slabs.append(lax.ppermute(shared, 'y', ring(-step, Y_SIZE)))  23.1 us
    all_to_all x3, starting transfers between devices, local(): arrived = lax.all_to_all(picked, PLANE, 0, 0, tiled=True)  17.6 us
    pallas_call x1, Pallas kernels, solve(): pl.pallas_call(solve_kernel, name='solve', grid_spec=pltpu.PrefetchScalar...  16.1 us
    all_to_all x3, waiting for transfers between devices, local(): arrived = lax.all_to_all(picked, PLANE, 0, 0, tiled=True)  15.3 us
    ppermute x3, waiting for transfers between devices, local(): up = lax.ppermute(up, 'z', ring(1))  13.4 us
    pallas_call x1, Pallas kernels, warm(): pl.pallas_call(warm_kernel, name='warm', grid_spec=pltpu.PrefetchScalarGr...  13.1 us
    ppermute x3, waiting for transfers between devices, local(): same.append(lax.ppermute(merged, 'user', line(-step)))  10.2 us
    ppermute x3, starting transfers between devices, local(): down = lax.ppermute(down, 'z', ring(-1))  9.36 us
  transfers between devices with their start and end apart: 18, of which 12 were waited for; matrix products, arithmetic and copies ran while one was open for 2% of the time, Pallas kernels for 11%

profile of v3, /device:TPU:1, one launch (start us, length us, event | category | flops | bytes accessed | tf_op | source)
XLA Modules:
  0.0 168.6 jit_solution(16376985860600442513)
XLA Ops:
  3.0 2.5 %collective-permute-start = (bf16[18,32,256]{2,1,0:T(8,128)(2,1)S(1)}, bf16[18,32,256]{2,1,0:T(8,128)(2,1)S(1)}, u32[]{:S(2)}, u32[]{:S(2)}) collective-permute-start(bf16[18,32,256]{2,1,0:T(8,128)(2,1)S(1)} %prepare.1.refs_0_), channel_id=1, source_target_pairs={{0,1},{1,2},{2,3},{3,4},{4,5},{5,6},{6,7},{7,0},{8,9},{9,10},{10,1... | collective-permute-start | bytes 884744 | tf_op jit(solution)/shard_map/ppermute | solution.py:433
  5.5 4.0 %collective-permute-start.1 = (bf16[18,32,256]{2,1,0:T(8,128)(2,1)S(1)}, bf16[18,32,256]{2,1,0:T(8,128)(2,1)S(1)}, u32[]{:S(2)}, u32[]{:S(2)}) collective-permute-start(bf16[18,32,256]{2,1,0:T(8,128)(2,1)S(1)} %prepare.1.refs_0_), channel_id=1, source_target_pairs={{0,7},{1,0},{2,1},{3,2},{4,3},{5,4},{6,5},{7,6},{8,15},{9,8},{10,9... | collective-permute-start | bytes 884744 | tf_op jit(solution)/shard_map/ppermute | solution.py:434
  9.6 6.6 %collective-permute-done.refs_1_ = bf16[18,32,256]{2,1,0:T(8,128)(2,1)S(1)} collective-permute-done((bf16[18,32,256]{2,1,0:T(8,128)(2,1)S(1)}, bf16[18,32,256]{2,1,0:T(8,128)(2,1)S(1)}, u32[]{:S(2)}, u32[]{:S(2)}) %collective-permute-start) | collective-permute-done | bytes 294944 | tf_op jit(solution)/shard_map/ppermute | solution.py:433
  16.2 2.7 %collective-permute-start.3 = (bf16[18,32,256]{2,1,0:T(8,128)(2,1)S(1)}, bf16[18,32,256]{2,1,0:T(8,128)(2,1)S(1)}, u32[]{:S(2)}, u32[]{:S(2)}) collective-permute-start(bf16[18,32,256]{2,1,0:T(8,128)(2,1)S(1)} %collective-permute-done.1.refs_2_), channel_id=1, source_target_pairs={{0,7},{1,0},{2,1},{3,2},{4,3},{5,4},{6,5},{7,6},{8,15},{9,8},{10,9... | collective-permute-start | bytes 884744 | tf_op jit(solution)/shard_map/ppermute | solution.py:434
  19.7 8.9 %all-to-all-start = ((s32[32,1,8]{2,1,0:T(1,128)}), s32[32,1,8]{2,1,0:T(1,128)S(1)}, u32[]{:S(2)}, u32[]{:S(2)}) async-start(s32[32,1,8]{2,1,0:T(1,128)} %bitcast.5), calls=%async_computation | async-start | bytes 32768 | tf_op jit(solution)/shard_map/all_to_all | solution.py:428
  28.6 6.9 %all-to-all-done = s32[32,1,8]{2,1,0:T(1,128)S(1)} async-done(((s32[32,1,8]{2,1,0:T(1,128)}), s32[32,1,8]{2,1,0:T(1,128)S(1)}, u32[]{:S(2)}, u32[]{:S(2)}) %all-to-all-start) | async-done | bytes 1056 | tf_op jit(solution)/shard_map/all_to_all | solution.py:428
  37.3 4.2 %all-to-all-start.2 = ((bf16[32,64,256]{2,1,0:T(8,128)(2,1)}), bf16[32,64,256]{2,1,0:T(8,128)(2,1)S(1)}, u32[]{:S(2)}, u32[]{:S(2)}) async-start(bf16[32,64,256]{2,1,0:T(8,128)(2,1)} %pick.4), calls=%async_computation.2 | async-start | bytes 2097152 | tf_op jit(solution)/shard_map/all_to_all | solution.py:441
  41.6 2.2 %pick.3 = bf16[32,96,256]{2,1,0:T(8,128)(2,1)} custom-call(s32[32,8]{1,0:T(8,128)S(1)} %bitcast.45, s32[1]{0:T(128)} %bitcast.7.place, bf16[18,32,256]{2,1,0:T(8,128)(2,1)S(1)} %prepare.1.refs_0_, bf16[18,32,256]{2,1,0:T(8,128)(2,1)S(1)} %collective-permute-done.refs_1_, bf16[18,32,256]{2,1,0:T(8,128)(2,1)S(1)} %collective-permute-done.1.refs_2_), custom_call_target="tpu_custom_call" | custom-call | tf_op jit(solution)/shard_map/pick/pallas_call | solution.py:87
  43.8 14.2 %all-to-all-done.2 = bf16[32,64,256]{2,1,0:T(8,128)(2,1)S(1)} async-done(((bf16[32,64,256]{2,1,0:T(8,128)(2,1)}), bf16[32,64,256]{2,1,0:T(8,128)(2,1)S(1)}, u32[]{:S(2)}, u32[]{:S(2)}) %all-to-all-start.2) | async-done | bytes 1048608 | tf_op jit(solution)/shard_map/all_to_all | solution.py:441
  57.9 5.4 %all-to-all-start.1 = ((bf16[32,96,256]{2,1,0:T(8,128)(2,1)}), bf16[32,96,256]{2,1,0:T(8,128)(2,1)}, u32[]{:S(2)}, u32[]{:S(2)}) async-start(bf16[32,96,256]{2,1,0:T(8,128)(2,1)} %pick.3), calls=%async_computation.1 | async-start | bytes 3145728 | tf_op jit(solution)/shard_map/all_to_all | solution.py:441
  63.4 2.7 %collective-permute-start.5 = (bf16[18,32,256]{2,1,0:T(8,128)(2,1)S(1)}, bf16[18,32,256]{2,1,0:T(8,128)(2,1)S(1)}, u32[]{:S(2)}, u32[]{:S(2)}) collective-permute-start(bf16[18,32,256]{2,1,0:T(8,128)(2,1)S(1)} %collective-permute-done.3.refs_1_.refs_4_), channel_id=1, source_target_pairs={{0,7},{1,0},{2,1},{3,2},{4,3},{5,4},{6,5},{7,6},{8,15},{9,8},{10,9... | collective-permute-start | bytes 884744 | tf_op jit(solution)/shard_map/ppermute | solution.py:434
  66.0 6.8 %collective-permute-done.4.refs_5_.refs_0_ = bf16[18,32,256]{2,1,0:T(8,128)(2,1)S(1)} collective-permute-done((bf16[18,32,256]{2,1,0:T(8,128)(2,1)S(1)}, bf16[18,32,256]{2,1,0:T(8,128)(2,1)S(1)}, u32[]{:S(2)}, u32[]{:S(2)}) %collective-permute-start.4) | collective-permute-done | bytes 294944 | tf_op jit(solution)/shard_map/ppermute | solution.py:433
  72.9 8.7 %collective-permute-done.6.refs_7_.refs_2_ = bf16[18,32,256]{2,1,0:T(8,128)(2,1)S(1)} collective-permute-done((bf16[18,32,256]{2,1,0:T(8,128)(2,1)S(1)}, bf16[18,32,256]{2,1,0:T(8,128)(2,1)S(1)}, u32[]{:S(2)}, u32[]{:S(2)}) %collective-permute-start.6) | collective-permute-done | bytes 294944 | tf_op jit(solution)/shard_map/ppermute | solution.py:436
  81.6 2.1 %pick.5 = bf16[32,96,256]{2,1,0:T(8,128)(2,1)} custom-call(s32[32,8]{1,0:T(8,128)S(1)} %bitcast.46, s32[1]{0:T(128)} %bitcast.7.place, bf16[18,32,256]{2,1,0:T(8,128)(2,1)S(1)} %collective-permute-done.4.refs_5_.refs_0_, bf16[18,32,256]{2,1,0:T(8,128)(2,1)S(1)} %collective-permute-done.5.refs_6_.refs_1_, ...), custom_call_target="tpu_custom_call" | custom-call | tf_op jit(solution)/shard_map/pick/pallas_call | solution.py:87
  84.8 8.0 %all-to-all-start.3 = ((bf16[32,96,256]{2,1,0:T(8,128)(2,1)}), bf16[32,96,256]{2,1,0:T(8,128)(2,1)}, u32[]{:S(2)}, u32[]{:S(2)}) async-start(bf16[32,96,256]{2,1,0:T(8,128)(2,1)} %pick.5), calls=%async_computation.3 | async-start | bytes 3145728 | tf_op jit(solution)/shard_map/all_to_all | solution.py:441
  93.8 2.6 %collective-permute-start.7 = (bf16[10,32,256]{2,1,0:T(8,128)(2,1)S(1)}, bf16[10,32,256]{2,1,0:T(8,128)(2,1)S(1)}, u32[]{:S(2)}, u32[]{:S(2)}) collective-permute-start(bf16[10,32,256]{2,1,0:T(8,128)(2,1)S(1)} %gather_heads.1.own), channel_id=1, source_target_pairs={{0,24},{8,0},{16,8},{24,16},{1,25},{9,1},{17,9},{25,17},{2,26},{10... | collective-permute-start | bytes 491528 | tf_op jit(solution)/shard_map/ppermute | solution.py:447
  97.6 18.2 %collective-permute-done.7.above = bf16[10,32,256]{2,1,0:T(8,128)(2,1)S(1)} collective-permute-done((bf16[10,32,256]{2,1,0:T(8,128)(2,1)S(1)}, bf16[10,32,256]{2,1,0:T(8,128)(2,1)S(1)}, u32[]{:S(2)}, u32[]{:S(2)}) %collective-permute-start.7) | collective-permute-done | bytes 163872 | tf_op jit(solution)/shard_map/ppermute | solution.py:447
  117.2 3.5 %collective-permute-done.9.below = bf16[10,32,256]{2,1,0:T(8,128)(2,1)S(1)} collective-permute-done((bf16[10,32,256]{2,1,0:T(8,128)(2,1)S(1)}, bf16[10,32,256]{2,1,0:T(8,128)(2,1)S(1)}, u32[]{:S(2)}, u32[]{:S(2)}) %collective-permute-start.9) | collective-permute-done | bytes 163872 | tf_op jit(solution)/shard_map/ppermute | solution.py:447
  121.5 2.1 %collective-permute-start.10 = (bf16[10,32,256]{2,1,0:T(8,128)(2,1)S(1)}, bf16[10,32,256]{2,1,0:T(8,128)(2,1)S(1)}, u32[]{:S(2)}, u32[]{:S(2)}) collective-permute-start(bf16[10,32,256]{2,1,0:T(8,128)(2,1)S(1)} %merge.1), channel_id=1, source_target_pairs={{0,192},{32,224},{64,0},{96,32},{128,64},{160,96},{192,128},{224,1... | collective-permute-start | bytes 491528 | tf_op jit(solution)/shard_map/ppermute | solution.py:451
  124.6 2.2 %collective-permute-done.10 = bf16[10,32,256]{2,1,0:T(8,128)(2,1)S(1)} collective-permute-done((bf16[10,32,256]{2,1,0:T(8,128)(2,1)S(1)}, bf16[10,32,256]{2,1,0:T(8,128)(2,1)S(1)}, u32[]{:S(2)}, u32[]{:S(2)}) %collective-permute-start.10) | collective-permute-done | bytes 163872 | tf_op jit(solution)/shard_map/ppermute | solution.py:451
  126.8 3.2 %collective-permute-done.11 = bf16[10,32,256]{2,1,0:T(8,128)(2,1)S(1)} collective-permute-done((bf16[10,32,256]{2,1,0:T(8,128)(2,1)S(1)}, bf16[10,32,256]{2,1,0:T(8,128)(2,1)S(1)}, u32[]{:S(2)}, u32[]{:S(2)}) %collective-permute-start.11) | collective-permute-done | bytes 163872 | tf_op jit(solution)/shard_map/ppermute | solution.py:451
  130.0 4.7 %collective-permute-done.12 = bf16[10,32,256]{2,1,0:T(8,128)(2,1)S(1)} collective-permute-done((bf16[10,32,256]{2,1,0:T(8,128)(2,1)S(1)}, bf16[10,32,256]{2,1,0:T(8,128)(2,1)S(1)}, u32[]{:S(2)}, u32[]{:S(2)}) %collective-permute-start.12) | collective-permute-done | bytes 163872 | tf_op jit(solution)/shard_map/ppermute | solution.py:451
  139.2 13.1 %warm.1 = (bf16[256,6144]{1,0:T(8,128)(2,1)}, bf16[24,8,32,256]{3,2,1,0:T(8,128)(2,1)}, bf16[2,8,32,256]{3,2,1,0:T(8,128)(2,1)}, f32[256,256]{1,0:T(8,128)}) custom-call(s32[16]{0:T(128)} %get-tuple-element.10.order, s32[16]{0:T(128)} %get-tuple-element.12.slab, s32[16]{0:T(128)} %get-tuple-element.11.slot, s32[1]{0:T(128)} %bitcast.3.early, ...), custom_call_target="tpu_custom_call" | custom-call | tf_op jit(solution)/shard_map/warm/pallas_call | solution.py:266
  152.3 16.1 %solve.1 = (f32[256,256]{1,0:T(8,128)}, f32[256,256]{1,0:T(8,128)}) custom-call(s32[16]{0:T(128)} %get-tuple-element.12.slab, s32[16]{0:T(128)} %get-tuple-element.11.slot, s32[1]{0:T(128)} %bitcast.3.early, f32[256,256]{1,0:T(8,128)} %start.3, bf16[256,6144]{1,0:T(8,128)(2,1)} %get-tuple-element.6.weights_in, ...), custom_call_target="tpu_custom_call" | custom-call | tf_op jit(solution)/shard_map/solve/pallas_call | solution.py:387
  (47 shorter events, 15.2 us)
Async XLA Ops:
  0.6 18.2 %copy-start.6 = (s32[1,16]{1,0:T(1,128)S(1)}, s32[1,16]{1,0:T(1,128)}, u32[]{:S(2)}) copy-start(s32[1,16]{1,0:T(1,128)} %param.10) | copy-start | bytes 196
  0.6 1.6 copy-start
  3.0 13.2 %collective-permute-start = (bf16[18,32,256]{2,1,0:T(8,128)(2,1)S(1)}, bf16[18,32,256]{2,1,0:T(8,128)(2,1)S(1)}, u32[]{:S(2)}, u32[]{:S(2)}) collective-permute-start(bf16[18,32,256]{2,1,0:T(8,128)(2,1)S(1)} %prepare.1.refs_0_), channel_id=1, source_target_pairs={{0,1},{1,2},{2,3},{3,4},{4,5},{5,6},{6,7},{7,0},{8,9},{9,10},{10,1... | collective-permute-start | bytes 884744 | tf_op jit(solution)/shard_map/ppermute | solution.py:433
  5.5 10.7 %collective-permute-start.1 = (bf16[18,32,256]{2,1,0:T(8,128)(2,1)S(1)}, bf16[18,32,256]{2,1,0:T(8,128)(2,1)S(1)}, u32[]{:S(2)}, u32[]{:S(2)}) collective-permute-start(bf16[18,32,256]{2,1,0:T(8,128)(2,1)S(1)} %prepare.1.refs_0_), channel_id=1, source_target_pairs={{0,7},{1,0},{2,1},{3,2},{4,3},{5,4},{6,5},{7,6},{8,15},{9,8},{10,9... | collective-permute-start | bytes 884744 | tf_op jit(solution)/shard_map/ppermute | solution.py:434
  16.2 19.3 %collective-permute-start.2 = (bf16[18,32,256]{2,1,0:T(8,128)(2,1)S(1)}, bf16[18,32,256]{2,1,0:T(8,128)(2,1)S(1)}, u32[]{:S(2)}, u32[]{:S(2)}) collective-permute-start(bf16[18,32,256]{2,1,0:T(8,128)(2,1)S(1)} %collective-permute-done.refs_1_), channel_id=1, source_target_pairs={{0,1},{1,2},{2,3},{3,4},{4,5},{5,6},{6,7},{7,0},{8,9},{9,10},{10,1... | collective-permute-start | bytes 884744 | tf_op jit(solution)/shard_map/ppermute | solution.py:433
  16.2 19.3 %collective-permute-start.3 = (bf16[18,32,256]{2,1,0:T(8,128)(2,1)S(1)}, bf16[18,32,256]{2,1,0:T(8,128)(2,1)S(1)}, u32[]{:S(2)}, u32[]{:S(2)}) collective-permute-start(bf16[18,32,256]{2,1,0:T(8,128)(2,1)S(1)} %collective-permute-done.1.refs_2_), channel_id=1, source_target_pairs={{0,7},{1,0},{2,1},{3,2},{4,3},{5,4},{6,5},{7,6},{8,15},{9,8},{10,9... | collective-permute-start | bytes 884744 | tf_op jit(solution)/shard_map/ppermute | solution.py:434
  19.7 15.8 %all-to-all-start = ((s32[32,1,8]{2,1,0:T(1,128)}), s32[32,1,8]{2,1,0:T(1,128)S(1)}, u32[]{:S(2)}, u32[]{:S(2)}) async-start(s32[32,1,8]{2,1,0:T(1,128)} %bitcast.5), calls=%async_computation | async-start | bytes 32768 | tf_op jit(solution)/shard_map/all_to_all | solution.py:428
  37.3 20.6 %all-to-all-start.2 = ((bf16[32,64,256]{2,1,0:T(8,128)(2,1)}), bf16[32,64,256]{2,1,0:T(8,128)(2,1)S(1)}, u32[]{:S(2)}, u32[]{:S(2)}) async-start(bf16[32,64,256]{2,1,0:T(8,128)(2,1)} %pick.4), calls=%async_computation.2 | async-start | bytes 2097152 | tf_op jit(solution)/shard_map/all_to_all | solution.py:441
  57.9 25.8 %copy-start.3 = (bf16[32,64,256]{2,1,0:T(8,128)(2,1)}, bf16[32,64,256]{2,1,0:T(8,128)(2,1)S(1)}, u32[]{:S(2)}) copy-start(bf16[32,64,256]{2,1,0:T(8,128)(2,1)S(1)} %all-to-all-done.2) | copy-start | bytes 3145732
  57.9 26.9 %all-to-all-start.1 = ((bf16[32,96,256]{2,1,0:T(8,128)(2,1)}), bf16[32,96,256]{2,1,0:T(8,128)(2,1)}, u32[]{:S(2)}, u32[]{:S(2)}) async-start(bf16[32,96,256]{2,1,0:T(8,128)(2,1)} %pick.3), calls=%async_computation.1 | async-start | bytes 3145728 | tf_op jit(solution)/shard_map/all_to_all | solution.py:441
  63.3 9.6 %collective-permute-start.4 = (bf16[18,32,256]{2,1,0:T(8,128)(2,1)S(1)}, bf16[18,32,256]{2,1,0:T(8,128)(2,1)S(1)}, u32[]{:S(2)}, u32[]{:S(2)}) collective-permute-start(bf16[18,32,256]{2,1,0:T(8,128)(2,1)S(1)} %collective-permute-done.2.refs_0_.refs_3_), channel_id=1, source_target_pairs={{0,1},{1,2},{2,3},{3,4},{4,5},{5,6},{6,7},{7,0},{8,9},{9,10},{10,1... | collective-permute-start | bytes 884744 | tf_op jit(solution)/shard_map/ppermute | solution.py:433
  63.4 9.5 %collective-permute-start.5 = (bf16[18,32,256]{2,1,0:T(8,128)(2,1)S(1)}, bf16[18,32,256]{2,1,0:T(8,128)(2,1)S(1)}, u32[]{:S(2)}, u32[]{:S(2)}) collective-permute-start(bf16[18,32,256]{2,1,0:T(8,128)(2,1)S(1)} %collective-permute-done.3.refs_1_.refs_4_), channel_id=1, source_target_pairs={{0,7},{1,0},{2,1},{3,2},{4,3},{5,4},{6,5},{7,6},{8,15},{9,8},{10,9... | collective-permute-start | bytes 884744 | tf_op jit(solution)/shard_map/ppermute | solution.py:434
  72.9 8.7 %collective-permute-start.6 = (bf16[18,32,256]{2,1,0:T(8,128)(2,1)S(1)}, bf16[18,32,256]{2,1,0:T(8,128)(2,1)S(1)}, u32[]{:S(2)}, u32[]{:S(2)}) collective-permute-start(bf16[18,32,256]{2,1,0:T(8,128)(2,1)S(1)} %collective-permute-done.4.refs_5_.refs_0_), channel_id=1, source_target_pairs={{0,1},{1,2},{2,3},{3,4},{4,5},{5,6},{6,7},{7,0},{8,9},{9,10},{10,1... | collective-permute-start | bytes 884744 | tf_op jit(solution)/shard_map/ppermute | solution.py:436
  83.7 9.1 %copy-start.1 = (s32[8]{0:T(128)S(1)}, s32[8]{0:T(128)}, u32[]{:S(2)}) copy-start(s32[8]{0:T(128)} %head_ids.1) | copy-start | bytes 100
  84.8 67.5 %all-to-all-start.3 = ((bf16[32,96,256]{2,1,0:T(8,128)(2,1)}), bf16[32,96,256]{2,1,0:T(8,128)(2,1)}, u32[]{:S(2)}, u32[]{:S(2)}) async-start(bf16[32,96,256]{2,1,0:T(8,128)(2,1)} %pick.5), calls=%async_computation.3 | async-start | bytes 3145728 | tf_op jit(solution)/shard_map/all_to_all | solution.py:441
  92.8 42.6 %copy-start.2 = (s32[8]{0:T(128)S(1)}, s32[8]{0:T(128)}, u32[]{:S(2)}) copy-start(s32[8]{0:T(128)} %constant.81.clone) | copy-start | bytes 100
  93.8 22.0 %collective-permute-start.7 = (bf16[10,32,256]{2,1,0:T(8,128)(2,1)S(1)}, bf16[10,32,256]{2,1,0:T(8,128)(2,1)S(1)}, u32[]{:S(2)}, u32[]{:S(2)}) collective-permute-start(bf16[10,32,256]{2,1,0:T(8,128)(2,1)S(1)} %gather_heads.1.own), channel_id=1, source_target_pairs={{0,24},{8,0},{16,8},{24,16},{1,25},{9,1},{17,9},{25,17},{2,26},{10... | collective-permute-start | bytes 491528 | tf_op jit(solution)/shard_map/ppermute | solution.py:447
  96.5 20.8 %collective-permute-start.8 = (bf16[10,32,256]{2,1,0:T(8,128)(2,1)S(1)}, bf16[10,32,256]{2,1,0:T(8,128)(2,1)S(1)}, u32[]{:S(2)}, u32[]{:S(2)}) collective-permute-start(bf16[10,32,256]{2,1,0:T(8,128)(2,1)S(1)} %gather_heads.1.own), channel_id=1, source_target_pairs={{0,16},{8,24},{16,0},{24,8},{1,17},{9,25},{17,1},{25,9},{2,18},{10... | collective-permute-start | bytes 491528 | tf_op jit(solution)/shard_map/ppermute | solution.py:447
  97.0 23.7 %collective-permute-start.9 = (bf16[10,32,256]{2,1,0:T(8,128)(2,1)S(1)}, bf16[10,32,256]{2,1,0:T(8,128)(2,1)S(1)}, u32[]{:S(2)}, u32[]{:S(2)}) collective-permute-start(bf16[10,32,256]{2,1,0:T(8,128)(2,1)S(1)} %gather_heads.1.own), channel_id=1, source_target_pairs={{0,8},{8,16},{16,24},{24,0},{1,9},{9,17},{17,25},{25,1},{2,10},{10... | collective-permute-start | bytes 491528 | tf_op jit(solution)/shard_map/ppermute | solution.py:447
  121.5 5.3 %collective-permute-start.10 = (bf16[10,32,256]{2,1,0:T(8,128)(2,1)S(1)}, bf16[10,32,256]{2,1,0:T(8,128)(2,1)S(1)}, u32[]{:S(2)}, u32[]{:S(2)}) collective-permute-start(bf16[10,32,256]{2,1,0:T(8,128)(2,1)S(1)} %merge.1), channel_id=1, source_target_pairs={{0,192},{32,224},{64,0},{96,32},{128,64},{160,96},{192,128},{224,1... | collective-permute-start | bytes 491528 | tf_op jit(solution)/shard_map/ppermute | solution.py:451
  123.6 6.4 %collective-permute-start.11 = (bf16[10,32,256]{2,1,0:T(8,128)(2,1)S(1)}, bf16[10,32,256]{2,1,0:T(8,128)(2,1)S(1)}, u32[]{:S(2)}, u32[]{:S(2)}) collective-permute-start(bf16[10,32,256]{2,1,0:T(8,128)(2,1)S(1)} %merge.1), channel_id=1, source_target_pairs={{0,128},{32,160},{64,192},{96,224},{128,0},{160,32},{192,64},{224,... | collective-permute-start | bytes 491528 | tf_op jit(solution)/shard_map/ppermute | solution.py:451
  124.1 10.6 %collective-permute-start.12 = (bf16[10,32,256]{2,1,0:T(8,128)(2,1)S(1)}, bf16[10,32,256]{2,1,0:T(8,128)(2,1)S(1)}, u32[]{:S(2)}, u32[]{:S(2)}) collective-permute-start(bf16[10,32,256]{2,1,0:T(8,128)(2,1)S(1)} %merge.1), channel_id=1, source_target_pairs={{0,64},{32,96},{64,128},{96,160},{128,192},{160,224},{192,0},{224,... | collective-permute-start | bytes 491528 | tf_op jit(solution)/shard_map/ppermute | solution.py:451
  134.8 4.3 %copy-start.4 = (bf16[4,10,32,256]{3,2,1,0:T(8,128)(2,1)}, bf16[4,10,32,256]{3,2,1,0:T(8,128)(2,1)S(1)}, u32[]{:S(2)}) copy-start(bf16[4,10,32,256]{3,2,1,0:T(8,128)(2,1)S(1)} %pad_maximum_fusion.refs_2_) | copy-start | bytes 1966084
  134.8 3.4 %collective-permute-start.13 = (bf16[4,10,32,256]{3,2,1,0:T(8,128)(2,1)S(1)}, bf16[4,10,32,256]{3,2,1,0:T(8,128)(2,1)S(1)}, u32[]{:S(2)}, u32[]{:S(2)}) collective-permute-start(bf16[4,10,32,256]{3,2,1,0:T(8,128)(2,1)S(1)} %pad_maximum_fusion.refs_2_), channel_id=1, source_target_pairs={{0,32},{32,0},{64,96},{96,64},{128,160},{160,128},{192,224},{224,1... | collective-permute-start | bytes 1966088 | tf_op jit(solution)/shard_map/ppermute | solution.py:453
  (1 other events, 0.9 us)
